TPU v7x, 32 devices: a whole 2x2x4 slice. The times are simulated.
32 devices in a mesh: gx: 8 (over y, x, core), gz: 4 (over z).
Axes of the slice: x: 2, y: 2, z: 4, core: 2. Of those that a mesh axis runs over, the one named last changes fastest.
Arguments:
- velocity_old: float32 [3, 64, 64, 128], P(None, 'gx', 'gz'), may hold values from -6 to 6
- source: float32 [3, 64, 64, 128], P(None, 'gx', 'gz'), may hold values from -6 to 6
- diag_coef: float32 [64, 64, 128], P('gx', 'gz'), may hold values from 0.5 to 2
- face_coef: float32 [3, 64, 64, 128], P(None, 'gx', 'gz'), may hold values from 0.2 to 2
- bc_flags: int32 [2, 64, 64], P(None, 'gx', 'gz'), may hold values from 0 to 1
- coarse_map: int32 [64, 64, 128], P('gx', 'gz'), may hold values from 0 to 15
- coarse_inverse: float32 [512, 64], P('gx'), may hold values from -0.1 to 0.3
Outputs:
- velocity: float32 [3, 64, 64, 128], P(None, 'gx', 'gz')
- pressure: float32 [64, 64, 128], P('gx', 'gz')
All inputs are finite; a program needn't handle non-finite values.
Results may differ from a plain program's by a relative error of at most 0.0003.
Values sent between devices are 32-bit elements; how exact they have to be, the bound alone decides.
A program may use at most 64 MiB of HBM per device.

v0:
```python
import functools

import jax
import jax.numpy as jnp
from jax import lax
from jax.experimental import pallas as pl
from jax.experimental.pallas import tpu as pltpu
from jax.sharding import PartitionSpec as P

COARSE = 16
PAD = 8
DIRECT = 64

jacobi_weight = 2.0 / 3.0
MESH = pl.DeviceIdType.MESH


def kernel(
    dims,
    x0_in, src_in, diag_in, face_in, bc_in, map_in, inv_in,
    vel_ref, out_ref,
    x0_ref, src_ref, face_ref, bc_ref, map_ref, inv_ref,
    coef, res_ref, r_far, vk_ref, a1_ref, a2_ref, a3_ref,
    prs, pxlo, pxhi, pzlo, pzhi, pzsend,
    qxlo, qxhi, qzlo, qzhi, qzsend, qc_send, qc,
    mxlo, mxhi, mzlo, mzhi, mzsend, mc_send, mc,
    dxlo, dxhi, dzlo, dzhi, dzsend, inv_w, inv_e,
    msg, got, msg_z, got_z, msg_c, got_c, got_w, got_e,
    send_sem, recv_sem, near_s, near_r,
    sum_s, sum_r, sum_sz, sum_rz, coarse_s, coarse_r,
    load_sem, side_s, side_r,
):
    n_gx, n_gz, cx_n, cz_n, ny, lanes = dims
    rows = cx_n * cz_n
    deep = x0_ref.shape[2]
    gx = lax.axis_index("gx")
    gz = lax.axis_index("gz")
    east = (lax.rem(gx + 1, n_gx), gz)
    west = (lax.rem(gx + n_gx - 1, n_gx), gz)
    north = (gx, lax.rem(gz + 1, n_gz))
    south = (gx, lax.rem(gz + n_gz - 1, n_gz))
    row_x = [(lax.rem(gx + d, n_gx), gz) for d in range(1, n_gx)]
    row_z = [(gx, lax.rem(gz + d, n_gz)) for d in range(1, n_gz)]
    direct = n_gx * n_gz <= DIRECT
    pending = []

    def send(src, dst, ssem, rsem, to):
        copy = pltpu.make_async_remote_copy(
            src_ref=src, dst_ref=dst, send_sem=ssem, recv_sem=rsem,
            device_id=to, device_id_type=MESH,
        )
        copy.start()
        pending.append(copy)
        return copy

    aside_w = [(west[0], to[1]) for to in row_z]
    aside_e = [(east[0], to[1]) for to in row_z]
    corners = [
        (east[0], north[1]), (east[0], south[1]), (west[0], north[1]), (west[0], south[1])
    ]
    if direct:
        sum_to = [
            (lax.rem(gx + d, n_gx), lax.rem(gz + k, n_gz))
            for k in sorted(range(n_gz), key=lambda k: -min(k, n_gz - k))
            for d in sorted(range(n_gx), key=lambda d: -min(d, n_gx - d))
            if d or k
        ]
        partners = sum_to
    else:
        sum_to = row_x
        partners = row_x + row_z + aside_w + aside_e

    def inner(ref, halo):
        return ref.at[..., pl.ds(halo, cx_n), pl.ds(0, cz_n), :]

    loads = [
        pltpu.make_async_copy(a, b, load_sem.at[i])
        for i, (a, b) in enumerate(
            [
                (x0_in, inner(x0_ref, 2)), (face_in, inner(face_ref.at[pl.ds(0, 3)], 3)),
                (diag_in, inner(face_ref.at[3], 3)), (src_in, inner(src_ref, 1)),
                (bc_in, bc_ref), (map_in, map_ref), (inv_in, inv_ref),
            ]
        )
    ]
    for load in loads:
        load.start()
    barrier = pltpu.get_barrier_semaphore()
    for other in partners:
        pl.semaphore_signal(barrier, inc=1, device_id=other, device_id_type=MESH)
    for load in loads[:4]:
        load.wait()
    pl.semaphore_wait(barrier, len(partners))

    last = rows - cz_n

    def side_x(sign, halo, a, b):
        if sign > 0:
            return pl.ds(halo + cx_n - b, b - a + 1), pl.ds(halo - b, b - a + 1)
        return pl.ds(halo + a - 1, b - a + 1), pl.ds(halo + cx_n + a - 1, b - a + 1)

    def side_z(sign, a, b):
        if sign > 0:
            return pl.ds(cz_n - b, b - a + 1), pl.ds(deep - b, b - a + 1)
        return pl.ds(a - 1, b - a + 1), pl.ds(cz_n + a - 1, b - a + 1)

    used = []

    def ship(src, dst, to, where_from, where_to):
        i = len(used)
        used.append(i)
        return send(
            src.at[(..., *where_from, slice(None))], dst.at[(..., *where_to, slice(None))],
            near_s.at[i], near_r.at[i], to,
        )

    def to_corners(src, dst, halo, n):
        out = []
        for to, sx, sz in zip(corners, (1, 1, -1, -1), (1, -1, 1, -1)):
            (fx, tx), (fz, tz) = side_x(sx, halo, 1, n), side_z(sz, 1, n)
            out.append(ship(src, dst, to, (fx, fz), (tx, tz)))
        return out

    def to_z(src, dst, halo, a, b, ways=(1, -1)):
        out = []
        for sz in ways:
            fz, tz = side_z(sz, a, b)
            x = pl.ds(halo, cx_n)
            out.append(ship(src, dst, north if sz > 0 else south, (x, fz), (x, tz)))
        return out

    def to_x(src, dst, halo, a, b, ways=(1, -1)):
        out = []
        for sx in ways:
            fx, tx = side_x(sx, halo, a, b)
            z = pl.ds(0, cz_n)
            out.append(ship(src, dst, east if sx > 0 else west, (fx, z), (tx, z)))
        return out

    first = to_corners(x0_ref, x0_ref, 2, 1)
    first += to_corners(face_ref, face_ref, 3, 2)
    first += to_z(x0_ref, x0_ref, 2, 1, 2)
    first += to_z(face_ref, face_ref, 3, 1, 2)
    first += to_z(face_ref.at[1], face_ref.at[1], 3, 3, 3, (1,))
    first += to_z(src_ref, src_ref, 1, 1, 1)
    first += to_x(x0_ref, x0_ref, 2, 1, 2)
    first += to_x(face_ref, face_ref, 3, 1, 2)
    first += to_x(face_ref.at[0], face_ref.at[0], 3, 3, 3, (1,))
    first += to_x(src_ref, src_ref, 1, 1, 1)

    def exchange(phase, src, zs, lo_x, hi_x, lo_z, hi_z):
        zs[0] = src[:, pl.ds(cz_n - 1, cx_n, stride=cz_n), :]
        zs[1] = src[:, pl.ds(0, cx_n, stride=cz_n), :]
        sems = [(send_sem.at[phase, i], recv_sem.at[phase, i]) for i in range(4)]
        return [
            send(zs.at[0], lo_z, *sems[2], north),
            send(zs.at[1], hi_z, *sems[3], south),
            send(src.at[:, pl.ds(last, cz_n), :], lo_x, *sems[0], east),
            send(src.at[:, pl.ds(0, cz_n), :], hi_x, *sems[1], west),
        ]

    def exchange_pressure(i):
        return exchange(
            i, prs.at[i], pzsend.at[i], pxlo.at[i], pxhi.at[i], pzlo.at[i], pzhi.at[i]
        )

    def part(ref, which):
        return (slice(None),) * (len(ref.shape) - 2) + (which, slice(None))

    def exchange_wide(base, f, zs, cs, lo_x, hi_x, lo_z, hi_z, hold):
        sem = [(side_s.at[base + i], side_r.at[base + i]) for i in range(8)]
        for k, r in enumerate((rows - 1, last, cz_n - 1, 0)):
            cs[k] = f[part(f, pl.ds(r, 1))]
        for k in range(2):
            zs[0, k] = f[part(f, pl.ds(cz_n - 2 + k, cx_n, stride=cz_n))]
            zs[1, k] = f[part(f, pl.ds(k, cx_n, stride=cz_n))]
        copies = [
            send(cs.at[k], hold.at[k], *sem[k], to) for k, to in enumerate(corners)
        ]
        copies.append(send(zs.at[0], lo_z, *sem[4], north))
        copies.append(send(zs.at[1], hi_z, *sem[5], south))
        copies.append(send(f.at[part(f, pl.ds(last - cz_n, 2 * cz_n))], lo_x, *sem[6], east))
        copies.append(send(f.at[part(f, pl.ds(0, 2 * cz_n))], hi_x, *sem[7], west))
        return copies

    def arrive(copies):
        for copy in copies:
            copy.wait_recv()

    level = lax.broadcasted_iota(jnp.int32, (rows, ny), 1)
    depth = lax.rem(lax.broadcasted_iota(jnp.int32, (rows, ny), 0), cz_n)
    bottom = level == 0
    top = level == ny - 1
    front = depth == 0
    back = depth == cz_n - 1

    def spread(edge):
        wide = jnp.broadcast_to(edge[..., None, :], edge.shape[:-1] + (cz_n, ny))
        return wide.reshape(edge.shape[:-2] + (rows, ny))

    def x_prev(f, edge):
        return jnp.concatenate([edge, f[..., : rows - cz_n, :]], -2)

    def x_next(f, edge):
        return jnp.concatenate([f[..., cz_n:, :], edge], -2)

    def z_prev(f, edge):
        return jnp.where(front, spread(edge), pltpu.roll(f, 1, f.ndim - 2))

    def z_next(f, edge):
        return jnp.where(back, spread(edge), pltpu.roll(f, rows - 1, f.ndim - 2))

    def y_prev(f):
        return pltpu.roll(f, 1, f.ndim - 1)

    def y_next(f):
        return pltpu.roll(f, ny - 1, f.ndim - 1)

    eye = lax.broadcasted_iota(jnp.int32, (cz_n, cz_n), 0) == lax.broadcasted_iota(
        jnp.int32, (cz_n, cz_n), 1
    )

    def column(side):
        flags = bc_ref[side].astype(jnp.float32)
        parts = [
            jnp.sum(
                jnp.where(eye, jnp.broadcast_to(flags[i : i + 1], (cz_n, cz_n)), 0.0),
                axis=1, keepdims=True,
            )
            for i in range(cx_n)
        ]
        return jnp.broadcast_to(jnp.concatenate(parts, 0), (rows, ny))

    edge_rows = (cz_n, cz_n, cx_n, cx_n)
    around = ((0, 1), (2, 3), (0, 2), (1, 3))

    def insides(ref):
        return (
            ref[part(ref, pl.ds(0, cz_n))],
            ref[part(ref, pl.ds(last, cz_n))],
            ref[part(ref, pl.ds(0, cx_n, stride=cz_n))],
            ref[part(ref, pl.ds(cz_n - 1, cx_n, stride=cz_n))],
        )

    def split(lo_x, hi_x, lo_z, hi_z):
        near = (lo_x[..., cz_n:, :], hi_x[..., :cz_n, :], lo_z[1], hi_z[0])
        far = (lo_x[..., :cz_n, :], hi_x[..., cz_n:, :], lo_z[0], hi_z[1])
        return near, far

    def along_face(k, f, before, after):
        n = edge_rows[k]
        pos = lax.broadcasted_iota(jnp.int32, (n, ny), 0)
        return (
            jnp.where(pos == 0, before, pltpu.roll(f, 1, f.ndim - 2)),
            jnp.where(pos == n - 1, after, pltpu.roll(f, n - 1, f.ndim - 2)),
        )

    def scatter(msg, got, ssem, rsem, others):
        return [
            send(msg, got.at[d], ssem.at[d], rsem, to) for d, to in enumerate(others)
        ]

    def gathered(msg, got, rsem):
        pltpu.make_async_copy(got, got, rsem).wait()
        return msg[...] + jnp.sum(got[...], axis=0)


    def z_roll(f, shift):
        flat = f.reshape((-1,) + f.shape[-2:])
        return pltpu.roll(flat, shift % deep, 1).reshape(f.shape)

    def apply(f, c):
        h = (f.shape[0] - cx_n) // 2 - 1
        n = cx_n + 2 * h
        g = f[1:-1]
        total = coef[0, pl.ds(2 - h, n)] * g
        total -= face_ref[0, pl.ds(3 - h, n)] * f[2:] + face_ref[0, pl.ds(2 - h, n)] * f[:-2]
        total -= face_ref[1, pl.ds(3 - h, n)] * z_roll(g, -1) + coef[1, pl.ds(2 - h, n)] * z_roll(g, 1)
        total -= coef[2, pl.ds(2 - h, n)] * y_next(g) + coef[3, pl.ds(2 - h, n)] * y_prev(g)
        return total

    def own(f):
        h = (f.shape[0] - cx_n) // 2
        return f[h : h + cx_n, :cz_n].reshape(rows, ny)

    def pack(pairs):
        sums = [jnp.sum(a * b, axis=0, keepdims=True) for a, b in pairs]
        while len(sums) < 3 * PAD:
            sums.append(jnp.zeros_like(sums[0]))
        total = jnp.sum(jnp.concatenate(sums, 0), axis=1, keepdims=True)
        shape = (3 * PAD, 128)
        pick = lax.broadcasted_iota(jnp.int32, shape, 0) == lax.broadcasted_iota(
            jnp.int32, shape, 1
        )
        return jnp.sum(
            jnp.where(pick, jnp.broadcast_to(total, shape), 0.0), axis=0, keepdims=True
        )

    def sums_start(i, pairs):
        msg[i] = pack(pairs)
        scatter(msg.at[i], got.at[i], sum_s.at[i], sum_r.at[i], sum_to)

    def sums_end(i, count):
        total = gathered(msg.at[i], got.at[i], sum_r.at[i])
        if not direct:
            msg_z[i] = total
            scatter(msg_z.at[i], got_z.at[i], sum_sz.at[i], sum_rz.at[i], row_z)
            total = gathered(msg_z.at[i], got_z.at[i], sum_rz.at[i])
        shape = (8, 128)
        place = lax.broadcasted_iota(jnp.int32, shape, 0) * PAD
        lane = lax.broadcasted_iota(jnp.int32, shape, 1)
        wide = jnp.broadcast_to(total, shape)
        return [
            jnp.broadcast_to(
                jnp.sum(jnp.where(lane == place + k, wide, 0.0), axis=1, keepdims=True), shape
            )
            for k in range(count)
        ]

    slot = lax.broadcasted_iota(jnp.int32, (deep, ny), 0)
    floor = lax.broadcasted_iota(jnp.int32, (deep, ny), 1) == 0
    lid = lax.broadcasted_iota(jnp.int32, (deep, ny), 1) == ny - 1
    pdiag = 6.0 - jnp.where(bottom | top, 1.0, 0.0)
    loads[4].wait()
    pdiag = pdiag + jnp.where(bottom, column(0), 0.0) + jnp.where(top, column(1), 0.0)
    share = jacobi_weight / pdiag
    prs[4, 0] = pdiag
    loads[5].wait()
    loads[6].wait()

    arrive(first)
    for x in range(cx_n + 4):
        cx, cx_low = face_ref[0, x + 1], face_ref[0, x]
        cz, cy = face_ref[1, x + 1], face_ref[2, x + 1]
        cz_low = pltpu.roll(cz, 1, 0)
        upper = jnp.where(lid, 0.0, cy)
        lower = jnp.where(floor, 0.0, y_prev(cy))
        wall = jnp.where(floor | lid, jnp.broadcast_to(cy[:, ny - 1 :], (deep, ny)), 0.0)
        coef[0, x] = (face_ref[3, x + 1] + (cx + cz)) + ((upper + lower) + wall) + (cx_low + cz_low)
        coef[1, x] = cz_low
        coef[2, x] = upper
        coef[3, x] = lower

    dots = []
    for c in range(3):
        r = src_ref[c] - apply(x0_ref[c], c)
        res_ref[c] = r
        r_own = own(r)
        v = apply(r, c)
        v_own = own(v)
        vk_ref[c, pl.ds(3, cx_n), pl.ds(0, cz_n)] = v[:, :cz_n]
        dots.append([(r_own, r_own), (r_own, v_own)])
    second = to_corners(vk_ref, vk_ref, 3, 2)
    for to, sx, sz in zip(corners, (1, 1, -1, -1), (1, -1, 1, -1)):
        (fx, _), (fz, tz) = side_x(sx, 1, 1, 1), side_z(sz, 1, 1)
        second.append(ship(res_ref, r_far, to, (fx, fz), (side_x(sx, 2, 1, 1)[1], tz)))
    second += to_z(vk_ref, vk_ref, 3, 1, 3)
    for sz in (1, -1):
        fz, tz = side_z(sz, 2, 2)
        second.append(
            ship(res_ref, r_far, north if sz > 0 else south,
                 (pl.ds(1, cx_n), fz), (pl.ds(2, cx_n), tz))
        )
    second += to_x(vk_ref, vk_ref, 3, 1, 3)
    for sx in (1, -1):
        fx, tx = side_x(sx, 1, 2, 2)[0], side_x(sx, 2, 2, 2)[1]
        z = pl.ds(0, cz_n)
        second.append(ship(res_ref, r_far, east if sx > 0 else west, (fx, z), (tx, z)))
    zero = jnp.zeros((8, ny), jnp.float32)
    sums_start(0, [p for d in dots for p in d + [(zero, zero)] * (PAD - 2)])

    aside = exchange_wide(0, map_ref, mzsend, mc_send, mxlo, mxhi, mzlo, mzhi, mc)
    aside.append(send(inv_ref, inv_w, side_s.at[16], side_r.at[16], east))
    aside.append(send(inv_ref, inv_e, side_s.at[17], side_r.at[17], west))
    aside += exchange(3, prs.at[4], dzsend, dxlo, dxhi, dzlo, dzhi)

    arrive(second)
    m0, m1 = sums_end(0, 2)
    sigma = m1 / m0
    mine = (slot <= cz_n) | (slot == deep - 1)
    body_rows = slot < cz_n
    dots = []
    for c in range(3):
        s = sigma[c : c + 1]
        v = vk_ref[c]
        mid_r = jnp.where(mine, res_ref[c, pl.ds(1, cx_n)], r_far[c, pl.ds(2, cx_n)])
        lo_r = jnp.where(body_rows, res_ref[c, 0], r_far[c, 1])
        hi_r = jnp.where(body_rows, res_ref[c, cx_n + 1], r_far[c, cx_n + 2])
        r = jnp.concatenate(
            [r_far[c, pl.ds(0, 1)], lo_r[None], mid_r, hi_r[None], r_far[c, pl.ds(cx_n + 3, 1)]], 0
        )
        u = apply(v, c)
        v = v[1:-1]
        a1 = v - s * r
        a2 = (u - s * v) - s * a1
        a3 = apply(a2, c) - s * a2[1:-1]
        a4 = apply(a3, c) - s * a3[1:-1]
        r0, b1, b2, b3, b4 = own(r), own(a1), own(a2), own(a3), own(a4)
        dots += [
            (r0, b1), (b1, b1), (b1, b2), (b2, b2), (b2, b3), (b3, b3), (b3, b4), (b4, b4)
        ]
        a1_ref[c] = a1[1:-1]
        a2_ref[c] = a2[1:-1]
        a3_ref[c] = a3
    sums_start(1, dots)
    mu = [m0] + sums_end(1, PAD)

    def times(p):
        out = [sigma * p[0]]
        for i in range(1, len(p)):
            out.append(p[i - 1] + sigma * p[i])
        return out + [p[-1]]

    def dot(p, q):
        total = 0.0
        for n in range(len(p) + len(q) - 1):
            terms = [p[i] * q[n - i] for i in range(len(p)) if 0 <= n - i < len(q)]
            total = total + sum(terms[1:], terms[0]) * mu[n]
        return total

    def against(p):
        return sum((p[i] * mu[i] for i in range(1, len(p))), p[0] * mu[0])

    alpha = m0 / (sigma * m0 + mu[1])
    s1 = [1.0 - alpha * sigma, -alpha]
    t1 = times(s1)
    omega = dot(s1, t1) / dot(t1, t1)
    rho_new = against(s1) - omega * against(t1)
    beta = (rho_new / m0) * (alpha / omega)
    r1 = [s1[0] - omega * t1[0], s1[1] - omega * t1[1], -omega * t1[2]]
    p2 = [r1[0] + beta * (1.0 - omega * sigma), r1[1] - beta * omega, r1[2]]
    v2 = times(p2)
    alpha2 = rho_new / against(v2)
    s2 = [r1[i] - alpha2 * v2[i] for i in range(3)] + [-alpha2 * v2[3]]
    t2 = times(s2)
    omega2 = dot(s2, t2) / dot(t2, t2)
    weight = [
        alpha + omega * s1[0] + alpha2 * p2[0] + omega2 * s2[0],
        omega * s1[1] + alpha2 * p2[1] + omega2 * s2[1],
        alpha2 * p2[2] + omega2 * s2[2],
        omega2 * s2[3],
    ]
    speed = []
    for c in range(3):
        w = [k[c : c + 1] for k in weight]
        field = x0_ref[c, pl.ds(1, cx_n + 2)] + w[0] * res_ref[c]
        field += w[1] * a1_ref[c] + w[2] * a2_ref[c] + w[3] * a3_ref[c]
        vel_ref[c] = field[1:-1, :cz_n]
        speed.append(field)
    ux, uz, uy = speed
    div = (ux[1:-1] - ux[:-2]) + (uz[1:-1] - z_roll(uz[1:-1], 1))
    uy = uy[1:-1]
    div = div + (uy - jnp.where(floor, 0.0, y_prev(uy)))
    div = div[:, :cz_n].reshape(rows, ny)

    def operate(f, edges):
        near = x_next(f, edges[1]) + x_prev(f, edges[0])
        near += z_next(f, edges[3]) + z_prev(f, edges[2])
        near += jnp.where(top, 0.0, y_next(f)) + jnp.where(bottom, 0.0, y_prev(f))
        return pdiag * f - near

    def at_face(k, f, beyond, inside, before, after):
        lane = lax.broadcasted_iota(jnp.int32, f.shape, 1)
        before, after = along_face(k, f, before, after)
        near = (beyond + inside) + (before + after)
        near += jnp.where(lane == ny - 1, 0.0, y_next(f)) + jnp.where(lane == 0, 0.0, y_prev(f))
        return face_d[k] * f - near

    def operate_faces(ref, near, far, corner):
        return [
            at_face(k, near[k], far[k], inside, corner[around[k][0]], corner[around[k][1]])
            for k, inside in enumerate(insides(ref))
        ]

    q = share * div
    qref = prs.at[0, 0]
    qref[...] = q
    wide = exchange_wide(8, qref, qzsend, qc_send, qxlo, qxhi, qzlo, qzhi, qc)
    arrive(aside)
    face_d = (dxlo[0], dxhi[0], dzlo[0], dzhi[0])
    face_share = [jacobi_weight / d for d in face_d]
    arrive(wide)
    near, far = split(qxlo[...], qxhi[...], qzlo[...], qzhi[...])
    edges = [
        2.0 * near[k] - face_share[k] * out
        for k, out in enumerate(operate_faces(qref, near, far, [qc[k] for k in range(4)]))
    ]
    q = 2.0 * q - share * operate(q, near)
    res = div - operate(q, edges)
    cells = map_ref[...]
    parts = [
        jnp.sum(jnp.where(cells == m, res, 0.0), axis=0, keepdims=True) for m in range(COARSE)
    ]
    total = jnp.sum(jnp.concatenate(parts, 0), axis=1, keepdims=True)
    shape = (COARSE, lanes)
    place = lax.broadcasted_iota(jnp.int32, shape, 1) == (
        lax.broadcasted_iota(jnp.int32, shape, 0) + gz * COARSE
    )
    msg_c[...] = jnp.sum(
        jnp.where(place, jnp.broadcast_to(total, shape), 0.0), axis=0, keepdims=True
    )
    side = n_gz - 1
    scatter(msg_c, got_w, coarse_s.at[pl.ds(0, n_gz)], coarse_r.at[0], [east] + aside_e)
    scatter(msg_c, got_e, coarse_s.at[pl.ds(n_gz, n_gz)], coarse_r.at[1], [west] + aside_w)
    scatter(msg_c, got_c, coarse_s.at[pl.ds(2 * n_gz, side)], coarse_r.at[2], row_z)
    q = q + share * res
    prs[1, 0] = q
    halo = exchange_pressure(1)
    arrive(halo)
    q = q + share * (div - operate(q, (pxlo[1, 0], pxhi[1, 0], pzlo[1, 0], pzhi[1, 0])))

    spots = (south[1], gz, north[1])

    def corrections(inv, coarse):
        out = []
        for spot in spots:
            block = inv[pl.ds(pl.multiple_of(spot * COARSE, COARSE), COARSE), :]
            col = jnp.sum(block * coarse[:, : block.shape[1]], axis=1, keepdims=True)
            out.append(jnp.broadcast_to(col, (COARSE, ny)))
        return out

    def lift(cell, corr):
        add = jnp.broadcast_to(corr[0:1], cell.shape)
        for m in range(1, COARSE):
            add = jnp.where(cell == m, corr[m : m + 1], add)
        return add

    def whole(got, rsem):
        pltpu.make_async_copy(got, got, rsem).wait()
        return jnp.sum(got[...], axis=0)

    south_k, own_k, north_k = corrections(inv_ref, gathered(msg_c, got_c, coarse_r.at[2]))
    west_k = corrections(inv_w, whole(got_w, coarse_r.at[0]))
    east_k = corrections(inv_e, whole(got_e, coarse_r.at[1]))
    e = lift(cells, own_k)
    eref = prs.at[2, 0]
    eref[...] = e
    near, far = split(
        lift(mxlo[...], west_k[1]),
        lift(mxhi[...], east_k[1]),
        lift(mzlo[...], south_k),
        lift(mzhi[...], north_k),
    )
    points = [
        lift(mc[k], c) for k, c in enumerate((west_k[0], west_k[2], east_k[0], east_k[2]))
    ]
    edges = [
        near[k] - face_share[k] * out
        for k, out in enumerate(operate_faces(eref, near, far, points))
    ]
    e = e - share * operate(e, near)
    e = e - share * operate(e, edges)
    out_ref[...] = q + e
    for copy in pending:
        copy.wait_send()


def body(n_gx, n_gz, velocity_old, source, diag_coef, face_coef, bc_flags, coarse_map, coarse_inverse):
    cx_n, cz_n, ny = diag_coef.shape
    rows = cx_n * cz_n
    deep = cz_n + 8
    group = coarse_inverse.shape[1]
    lanes = -(-group // 128) * 128
    f32 = jnp.float32
    vmem = pltpu.VMEM
    dma = pltpu.SemaphoreType.DMA
    n_sum = n_gx * n_gz - 1 if n_gx * n_gz <= DIRECT else n_gx - 1

    def block(fields, halo):
        return vmem((fields, cx_n + 2 * halo, deep, ny), f32)

    def wide_set(kind):
        return [
            vmem((2 * cz_n, ny), kind),
            vmem((2 * cz_n, ny), kind),
            vmem((2, cx_n, ny), kind),
            vmem((2, cx_n, ny), kind),
            vmem((2, 2, cx_n, ny), kind),
            vmem((4, 1, ny), kind),
            vmem((4, 1, ny), kind),
        ]

    scratch = [
        block(3, 2),
        block(3, 1),
        block(4, 3),
        vmem(bc_flags.shape, jnp.int32),
        vmem((rows, ny), jnp.int32),
        vmem(coarse_inverse.shape, f32),
        block(4, 2),
        block(3, 1),
        block(3, 2),
        block(3, 3),
        block(3, 1),
        block(3, 1),
        block(3, 1),
        vmem((5, 1, rows, ny), f32),
        vmem((2, 1, cz_n, ny), f32),
        vmem((2, 1, cz_n, ny), f32),
        vmem((2, 1, cx_n, ny), f32),
        vmem((2, 1, cx_n, ny), f32),
        vmem((2, 2, 1, cx_n, ny), f32),
        *wide_set(f32),
        *wide_set(jnp.int32),
        vmem((1, cz_n, ny), f32),
        vmem((1, cz_n, ny), f32),
        vmem((1, cx_n, ny), f32),
        vmem((1, cx_n, ny), f32),
        vmem((2, 1, cx_n, ny), f32),
        vmem(coarse_inverse.shape, f32),
        vmem(coarse_inverse.shape, f32),
        vmem((2, 1, 128), f32),
        vmem((2, n_sum, 1, 128), f32),
        vmem((2, 1, 128), f32),
        vmem((2, n_gz - 1, 1, 128), f32),
        vmem((1, lanes), f32),
        vmem((n_gz - 1, 1, lanes), f32),
        vmem((n_gz, 1, lanes), f32),
        vmem((n_gz, 1, lanes), f32),
        dma((4, 4)),
        dma((4, 4)),
        dma((48,)),
        dma((48,)),
        dma((2, n_sum)),
        dma((2,)),
        dma((2, n_gz - 1)),
        dma((2,)),
        dma((3 * n_gz - 1,)),
        dma((3,)),
        dma((7,)),
        dma((18,)),
        dma((18,)),
    ]
    spec = pl.BlockSpec(memory_space=pltpu.VMEM)
    velocity, pressure = pl.pallas_call(
        functools.partial(kernel, (n_gx, n_gz, cx_n, cz_n, ny, lanes)),
        out_shape=(
            jax.ShapeDtypeStruct((3, cx_n, cz_n, ny), f32),
            jax.ShapeDtypeStruct((rows, ny), f32),
        ),
        in_specs=[pl.BlockSpec(memory_space=pltpu.HBM)] * 7,
        out_specs=(spec, spec),
        scratch_shapes=scratch,
        compiler_params=pltpu.CompilerParams(
            collective_id=0, has_side_effects=True, vmem_limit_bytes=48 * 1024 * 1024
        ),
        name="corrector",
    )(
        *[
            pltpu.with_memory_space_constraint(a, pltpu.HBM)
            for a in (
                velocity_old,
                source,
                diag_coef,
                face_coef,
                bc_flags,
                coarse_map.reshape(rows, ny),
                coarse_inverse,
            )
        ]
    )
    return velocity, pressure.reshape(cx_n, cz_n, ny)


def solution(mesh):
    placed = (
        P(None, "gx", "gz", None),
        P(None, "gx", "gz", None),
        P("gx", "gz", None),
        P(None, "gx", "gz", None),
        P(None, "gx", "gz"),
        P("gx", "gz", None),
        P("gx", None),
    )
    return jax.shard_map(
        functools.partial(body, mesh.shape["gx"], mesh.shape["gz"]),
        mesh=mesh,
        in_specs=placed,
        out_specs=(P(None, "gx", "gz", None), P("gx", "gz", None)),
        check_vma=False,
    )
```

profile of v0, /device:TPU:0, one launch (start us, length us, event | category | flops | bytes accessed | tf_op | source)
XLA Modules:
  0.0 38.7 jit_solution(12700229546051426536)
XLA Ops:
  0.6 36.7 %corrector.1 = (f32[3,8,16,128]{3,2,1,0:T(8,128)S(1)}, f32[128,128]{1,0:T(8,128)S(1)}) custom-call(f32[3,8,16,128]{3,2,1,0:T(8,128)} %x0_in.1, f32[3,8,16,128]{3,2,1,0:T(8,128)} %src_in.1, f32[8,16,128]{2,1,0:T(8,128)} %diag_in.1, f32[3,8,16,128]{3,2,1,0:T(8,128)} %face_in.1, s32[2,8,16]{2,1,0:T(8,128)} %bc_in.1, s32[128,128]{1,0:T(8,128)} %bitcast.3, ...), custom_call_target="tpu_custom_call" | custom-call | tf_op jit(solution)/shard_map/corrector/pallas_call | solution.py:635
  37.4 0.7 %copy.11 = f32[3,8,16,128]{3,2,1,0:T(8,128)} copy(f32[3,8,16,128]{3,2,1,0:T(8,128)S(1)} %get-tuple-element.8) | data formatting | bytes 393216
  38.0 0.6 %copy.12 = f32[8,16,128]{2,1,0:T(8,128)} copy(f32[8,16,128]{2,1,0:T(8,128)S(1)} %bitcast.2) | data formatting | bytes 131072
where the time goes:
time: 38.8 us; the launch traced here: 38.7 us
  Pallas kernels  36.7 us (95%)
  local copies, waits for them, and re-layouts  1.31 us (3%)
  between operations  0.64 us (2%)
    pallas_call x1, Pallas kernels, body(): pl.pallas_call(functools.partial(kernel, (n_gx, n_gz, cx_n, cz_n, ny, lan...  36.7 us
    unnamed x2, local copies, waits for them, and re-layouts  1.31 us

commit v1 on v0

--- a/solution.py
+++ b/solution.py
@@ -21,13 +21,9 @@
     vel_ref, out_ref,
     x0_ref, src_ref, face_ref, bc_ref, map_ref, inv_ref,
     coef, res_ref, r_far, vk_ref, a1_ref, a2_ref, a3_ref,
-    prs, pxlo, pxhi, pzlo, pzhi, pzsend,
-    qxlo, qxhi, qzlo, qzhi, qzsend, qc_send, qc,
-    mxlo, mxhi, mzlo, mzhi, mzsend, mc_send, mc,
-    dxlo, dxhi, dzlo, dzhi, dzsend, inv_w, inv_e,
-    msg, got, msg_z, got_z, msg_c, got_c, got_w, got_e,
-    send_sem, recv_sem, near_s, near_r,
-    sum_s, sum_r, sum_sz, sum_rz, coarse_s, coarse_r,
+    code_ref, cell_ref, pd_ref, share_ref, q_ref, inv_w, inv_e,
+    msg, got, msg_z, got_z, msg_c, got_c,
+    near_s, near_r, sum_s, sum_r, sum_sz, sum_rz, coarse_s, coarse_r,
     load_sem, side_s, side_r,
 ):
     n_gx, n_gz, cx_n, cz_n, ny, lanes = dims
@@ -53,22 +49,39 @@
         pending.append(copy)
         return copy
 
-    aside_w = [(west[0], to[1]) for to in row_z]
-    aside_e = [(east[0], to[1]) for to in row_z]
     corners = [
         (east[0], north[1]), (east[0], south[1]), (west[0], north[1]), (west[0], south[1])
     ]
+
+    def at(offset):
+        return (lax.rem(gx + offset[0], n_gx), lax.rem(gz + offset[1], n_gz))
+
+    def fold(d, k):
+        return (d % n_gx, k % n_gz)
+
+    around = {fold(d, k) for d in (-1, 0, 1) for k in (-1, 0, 1)} - {(0, 0)}
+    spread_to = sorted({fold(d, k) for d in range(-2, 3) for k in range(n_gz)} - {(0, 0)})
+    every = {(d, k) for d in range(n_gx) for k in range(n_gz)}
     if direct:
         sum_to = [
-            (lax.rem(gx + d, n_gx), lax.rem(gz + k, n_gz))
+            (d, k)
             for k in sorted(range(n_gz), key=lambda k: -min(k, n_gz - k))
             for d in sorted(range(n_gx), key=lambda d: -min(d, n_gx - d))
             if d or k
         ]
-        partners = sum_to
+        met = set(around)
+        while True:
+            seen = met | {fold(a + d, b + k) for a, b in around for d, k in met} | {(0, 0)}
+            left = sorted(every - seen, key=lambda o: (min(o[1], n_gz - o[1]), o))
+            if not left:
+                break
+            met |= {left[0], fold(-left[0][0], -left[0][1])}
+        sum_to = [at(o) for o in sum_to]
     else:
         sum_to = row_x
-        partners = row_x + row_z + aside_w + aside_e
+        met = around | set(spread_to)
+        met |= {(d, 0) for d in range(1, n_gx)} | {(0, k) for k in range(1, n_gz)}
+    partners = [at(o) for o in sorted(around)] + [at(o) for o in sorted(met - around)]
 
     def inner(ref, halo):
         return ref.at[..., pl.ds(halo, cx_n), pl.ds(0, cz_n), :]
@@ -92,7 +105,6 @@
         load.wait()
     pl.semaphore_wait(barrier, len(partners))
 
-    last = rows - cz_n
 
     def side_x(sign, halo, a, b):
         if sign > 0:
@@ -148,68 +160,13 @@
     first += to_x(face_ref.at[0], face_ref.at[0], 3, 3, 3, (1,))
     first += to_x(src_ref, src_ref, 1, 1, 1)
 
-    def exchange(phase, src, zs, lo_x, hi_x, lo_z, hi_z):
-        zs[0] = src[:, pl.ds(cz_n - 1, cx_n, stride=cz_n), :]
-        zs[1] = src[:, pl.ds(0, cx_n, stride=cz_n), :]
-        sems = [(send_sem.at[phase, i], recv_sem.at[phase, i]) for i in range(4)]
-        return [
-            send(zs.at[0], lo_z, *sems[2], north),
-            send(zs.at[1], hi_z, *sems[3], south),
-            send(src.at[:, pl.ds(last, cz_n), :], lo_x, *sems[0], east),
-            send(src.at[:, pl.ds(0, cz_n), :], hi_x, *sems[1], west),
-        ]
-
-    def exchange_pressure(i):
-        return exchange(
-            i, prs.at[i], pzsend.at[i], pxlo.at[i], pxhi.at[i], pzlo.at[i], pzhi.at[i]
-        )
-
-    def part(ref, which):
-        return (slice(None),) * (len(ref.shape) - 2) + (which, slice(None))
-
-    def exchange_wide(base, f, zs, cs, lo_x, hi_x, lo_z, hi_z, hold):
-        sem = [(side_s.at[base + i], side_r.at[base + i]) for i in range(8)]
-        for k, r in enumerate((rows - 1, last, cz_n - 1, 0)):
-            cs[k] = f[part(f, pl.ds(r, 1))]
-        for k in range(2):
-            zs[0, k] = f[part(f, pl.ds(cz_n - 2 + k, cx_n, stride=cz_n))]
-            zs[1, k] = f[part(f, pl.ds(k, cx_n, stride=cz_n))]
-        copies = [
-            send(cs.at[k], hold.at[k], *sem[k], to) for k, to in enumerate(corners)
-        ]
-        copies.append(send(zs.at[0], lo_z, *sem[4], north))
-        copies.append(send(zs.at[1], hi_z, *sem[5], south))
-        copies.append(send(f.at[part(f, pl.ds(last - cz_n, 2 * cz_n))], lo_x, *sem[6], east))
-        copies.append(send(f.at[part(f, pl.ds(0, 2 * cz_n))], hi_x, *sem[7], west))
-        return copies
-
     def arrive(copies):
         for copy in copies:
             copy.wait_recv()
 
     level = lax.broadcasted_iota(jnp.int32, (rows, ny), 1)
-    depth = lax.rem(lax.broadcasted_iota(jnp.int32, (rows, ny), 0), cz_n)
     bottom = level == 0
     top = level == ny - 1
-    front = depth == 0
-    back = depth == cz_n - 1
-
-    def spread(edge):
-        wide = jnp.broadcast_to(edge[..., None, :], edge.shape[:-1] + (cz_n, ny))
-        return wide.reshape(edge.shape[:-2] + (rows, ny))
-
-    def x_prev(f, edge):
-        return jnp.concatenate([edge, f[..., : rows - cz_n, :]], -2)
-
-    def x_next(f, edge):
-        return jnp.concatenate([f[..., cz_n:, :], edge], -2)
-
-    def z_prev(f, edge):
-        return jnp.where(front, spread(edge), pltpu.roll(f, 1, f.ndim - 2))
-
-    def z_next(f, edge):
-        return jnp.where(back, spread(edge), pltpu.roll(f, rows - 1, f.ndim - 2))
-
     def y_prev(f):
         return pltpu.roll(f, 1, f.ndim - 1)
 
@@ -221,39 +178,15 @@
     )
 
     def column(side):
-        flags = bc_ref[side].astype(jnp.float32)
+        flags = bc_ref[side]
         parts = [
             jnp.sum(
-                jnp.where(eye, jnp.broadcast_to(flags[i : i + 1], (cz_n, cz_n)), 0.0),
+                jnp.where(eye, jnp.broadcast_to(flags[i : i + 1], (cz_n, cz_n)), 0),
                 axis=1, keepdims=True,
             )
             for i in range(cx_n)
         ]
         return jnp.broadcast_to(jnp.concatenate(parts, 0), (rows, ny))
-
-    edge_rows = (cz_n, cz_n, cx_n, cx_n)
-    around = ((0, 1), (2, 3), (0, 2), (1, 3))
-
-    def insides(ref):
-        return (
-            ref[part(ref, pl.ds(0, cz_n))],
-            ref[part(ref, pl.ds(last, cz_n))],
-            ref[part(ref, pl.ds(0, cx_n, stride=cz_n))],
-            ref[part(ref, pl.ds(cz_n - 1, cx_n, stride=cz_n))],
-        )
-
-    def split(lo_x, hi_x, lo_z, hi_z):
-        near = (lo_x[..., cz_n:, :], hi_x[..., :cz_n, :], lo_z[1], hi_z[0])
-        far = (lo_x[..., :cz_n, :], hi_x[..., cz_n:, :], lo_z[0], hi_z[1])
-        return near, far
-
-    def along_face(k, f, before, after):
-        n = edge_rows[k]
-        pos = lax.broadcasted_iota(jnp.int32, (n, ny), 0)
-        return (
-            jnp.where(pos == 0, before, pltpu.roll(f, 1, f.ndim - 2)),
-            jnp.where(pos == n - 1, after, pltpu.roll(f, n - 1, f.ndim - 2)),
-        )
 
     def scatter(msg, got, ssem, rsem, others):
         return [
@@ -320,13 +253,11 @@
     slot = lax.broadcasted_iota(jnp.int32, (deep, ny), 0)
     floor = lax.broadcasted_iota(jnp.int32, (deep, ny), 1) == 0
     lid = lax.broadcasted_iota(jnp.int32, (deep, ny), 1) == ny - 1
-    pdiag = 6.0 - jnp.where(bottom | top, 1.0, 0.0)
-    loads[4].wait()
-    pdiag = pdiag + jnp.where(bottom, column(0), 0.0) + jnp.where(top, column(1), 0.0)
-    share = jacobi_weight / pdiag
-    prs[4, 0] = pdiag
-    loads[5].wait()
-    loads[6].wait()
+    for load in loads[4:]:
+        load.wait()
+    flag = jnp.where(bottom, column(0), 0) + jnp.where(top, column(1), 0)
+    code = map_ref[...] + COARSE * flag
+    code_ref[pl.ds(2, cx_n), pl.ds(0, cz_n)] = code.reshape(cx_n, cz_n, ny)
 
     arrive(first)
     for x in range(cx_n + 4):
@@ -369,10 +300,11 @@
     zero = jnp.zeros((8, ny), jnp.float32)
     sums_start(0, [p for d in dots for p in d + [(zero, zero)] * (PAD - 2)])
 
-    aside = exchange_wide(0, map_ref, mzsend, mc_send, mxlo, mxhi, mzlo, mzhi, mc)
-    aside.append(send(inv_ref, inv_w, side_s.at[16], side_r.at[16], east))
-    aside.append(send(inv_ref, inv_e, side_s.at[17], side_r.at[17], west))
-    aside += exchange(3, prs.at[4], dzsend, dxlo, dxhi, dzlo, dzhi)
+    aside = to_corners(code_ref, code_ref, 2, 1)
+    aside += to_z(code_ref, code_ref, 2, 1, 2)
+    aside += to_x(code_ref, code_ref, 2, 1, 2)
+    aside.append(send(inv_ref, inv_w, side_s.at[0], side_r.at[0], east))
+    aside.append(send(inv_ref, inv_e, side_s.at[1], side_r.at[1], west))
 
     arrive(second)
     m0, m1 = sums_end(0, 2)
@@ -403,6 +335,14 @@
         a2_ref[c] = a2[1:-1]
         a3_ref[c] = a3
     sums_start(1, dots)
+    arrive(aside)
+    for x in range(cx_n + 4):
+        mark = code_ref[x] >= COARSE
+        edge = floor | lid
+        pd = jnp.where(edge, jnp.where(mark, 6.0, 5.0), 6.0)
+        pd_ref[x] = pd
+        share_ref[x] = jacobi_weight / pd
+        cell_ref[x] = jnp.where(mark, code_ref[x] - COARSE, code_ref[x])
     mu = [m0] + sums_end(1, PAD)
 
     def times(p):
@@ -451,65 +391,84 @@
     div = (ux[1:-1] - ux[:-2]) + (uz[1:-1] - z_roll(uz[1:-1], 1))
     uy = uy[1:-1]
     div = div + (uy - jnp.where(floor, 0.0, y_prev(uy)))
-    div = div[:, :cz_n].reshape(rows, ny)
-
-    def operate(f, edges):
-        near = x_next(f, edges[1]) + x_prev(f, edges[0])
-        near += z_next(f, edges[3]) + z_prev(f, edges[2])
-        near += jnp.where(top, 0.0, y_next(f)) + jnp.where(bottom, 0.0, y_prev(f))
-        return pdiag * f - near
-
-    def at_face(k, f, beyond, inside, before, after):
-        lane = lax.broadcasted_iota(jnp.int32, f.shape, 1)
-        before, after = along_face(k, f, before, after)
-        near = (beyond + inside) + (before + after)
-        near += jnp.where(lane == ny - 1, 0.0, y_next(f)) + jnp.where(lane == 0, 0.0, y_prev(f))
-        return face_d[k] * f - near
-
-    def operate_faces(ref, near, far, corner):
-        return [
-            at_face(k, near[k], far[k], inside, corner[around[k][0]], corner[around[k][1]])
-            for k, inside in enumerate(insides(ref))
-        ]
-
+    share = share_ref[pl.ds(2, cx_n)]
     q = share * div
-    qref = prs.at[0, 0]
-    qref[...] = q
-    wide = exchange_wide(8, qref, qzsend, qc_send, qxlo, qxhi, qzlo, qzhi, qc)
-    arrive(aside)
-    face_d = (dxlo[0], dxhi[0], dzlo[0], dzhi[0])
-    face_share = [jacobi_weight / d for d in face_d]
-    arrive(wide)
-    near, far = split(qxlo[...], qxhi[...], qzlo[...], qzhi[...])
-    edges = [
-        2.0 * near[k] - face_share[k] * out
-        for k, out in enumerate(operate_faces(qref, near, far, [qc[k] for k in range(4)]))
+    q_ref[pl.ds(3, cx_n), pl.ds(0, cz_n)] = q[:, :cz_n]
+    third = to_corners(q_ref, q_ref, 3, 2)
+    third += to_z(q_ref, q_ref, 3, 1, 3)
+    third += to_x(q_ref, q_ref, 3, 1, 3)
+
+    def smooth(f):
+        n = f.shape[0] - 2
+        h = (n - cx_n) // 2
+        g = f[1:-1]
+        near = (f[2:] + f[:-2]) + (z_roll(g, 1) + z_roll(g, -1))
+        near += jnp.where(lid, 0.0, y_next(g)) + jnp.where(floor, 0.0, y_prev(g))
+        return pd_ref[pl.ds(2 - h, n)] * g - near
+
+    def shares(h):
+        return share_ref[pl.ds(2 - h, cx_n + 2 * h)]
+
+    blank = jnp.zeros((2, deep, ny), jnp.float32)
+    mine = jnp.where(body_rows, q, 0.0)
+    first_cut = -smooth(jnp.concatenate([blank, mine, blank], 0))
+    trace = jnp.concatenate(
+        [first_cut[:1], first_cut[1:-1] + jnp.where(body_rows, div, 0.0), first_cut[-1:]], 0
+    )
+    full = jnp.concatenate([blank[:1], trace, blank[:1]], 0)
+    full = full - smooth(jnp.concatenate([blank, shares(1) * trace, blank], 0))
+
+    part = [[] for _ in range(6)]
+    for m in range(COARSE):
+        hit = jnp.where(cell_ref[...] == m, full, 0.0)
+        flat = hit[:, :cz_n].reshape(-1, 8, ny)
+        step = cz_n // 8
+        top_rows = hit[:, cz_n:]
+        part[0].append(jnp.sum(flat[: 2 * step], axis=0, keepdims=True))
+        part[1].append(jnp.sum(flat[2 * step : -2 * step], axis=0, keepdims=True))
+        part[2].append(jnp.sum(flat[-2 * step :], axis=0, keepdims=True))
+        part[3].append(top_rows[1:2])
+        part[4].append(jnp.sum(top_rows[2:-2], axis=0, keepdims=True))
+        part[5].append(top_rows[-2:-1])
+    part = [jnp.concatenate(p, 0) for p in part]
+    upper_half = lax.broadcasted_iota(jnp.int32, (COARSE, 8, ny), 1) < 4
+
+    def total_of(p):
+        return jnp.sum(jnp.sum(p, axis=1), axis=1, keepdims=True)
+
+    shape = (COARSE, lanes)
+    spots = (south[1], gz, north[1])
+    places = [
+        lax.broadcasted_iota(jnp.int32, shape, 1)
+        == lax.broadcasted_iota(jnp.int32, shape, 0) + spot * COARSE
+        for spot in spots
     ]
-    q = 2.0 * q - share * operate(q, near)
-    res = div - operate(q, edges)
-    cells = map_ref[...]
-    parts = [
-        jnp.sum(jnp.where(cells == m, res, 0.0), axis=0, keepdims=True) for m in range(COARSE)
-    ]
-    total = jnp.sum(jnp.concatenate(parts, 0), axis=1, keepdims=True)
-    shape = (COARSE, lanes)
-    place = lax.broadcasted_iota(jnp.int32, shape, 1) == (
-        lax.broadcasted_iota(jnp.int32, shape, 0) + gz * COARSE
-    )
-    msg_c[...] = jnp.sum(
-        jnp.where(place, jnp.broadcast_to(total, shape), 0.0), axis=0, keepdims=True
-    )
-    side = n_gz - 1
-    scatter(msg_c, got_w, coarse_s.at[pl.ds(0, n_gz)], coarse_r.at[0], [east] + aside_e)
-    scatter(msg_c, got_e, coarse_s.at[pl.ds(n_gz, n_gz)], coarse_r.at[1], [west] + aside_w)
-    scatter(msg_c, got_c, coarse_s.at[pl.ds(2 * n_gz, side)], coarse_r.at[2], row_z)
-    q = q + share * res
-    prs[1, 0] = q
-    halo = exchange_pressure(1)
-    arrive(halo)
-    q = q + share * (div - operate(q, (pxlo[1, 0], pxhi[1, 0], pzlo[1, 0], pzhi[1, 0])))
-
-    spots = (south[1], gz, north[1])
+    for k in range(3):
+        cols = [
+            total_of(jnp.where(upper_half, 0.0, part[3 + k])), total_of(part[k]),
+            total_of(jnp.where(upper_half, part[3 + k], 0.0)),
+        ]
+        line = sum(
+            jnp.where(place, jnp.broadcast_to(col, shape), 0.0)
+            for place, col in zip(places, cols)
+        )
+        msg_c[k] = jnp.sum(line, axis=0, keepdims=True)
+    scatter(msg_c, got_c, coarse_s, coarse_r, [at(o) for o in spread_to])
+
+    arrive(third)
+    ext = q_ref[...]
+    q = 2.0 * ext[1:-1] - shares(2) * smooth(ext)
+    q = q[1:-1] + ext[2:-2] - shares(1) * smooth(q)
+    q = q[1:-1] + ext[3:-3] - shares(0) * smooth(q)
+
+    pltpu.make_async_copy(got_c, got_c, coarse_r).wait()
+
+    def restricted(t):
+        rows_in = [
+            got_c[spread_to.index(fold(-j, k)), t - j + 1]
+            for j in (t - 1, t, t + 1) for k in range(n_gz) if fold(-j, k) != (0, 0)
+        ]
+        return sum(rows_in, msg_c[t + 1])
 
     def corrections(inv, coarse):
         out = []
@@ -519,38 +478,27 @@
             out.append(jnp.broadcast_to(col, (COARSE, ny)))
         return out
 
-    def lift(cell, corr):
-        add = jnp.broadcast_to(corr[0:1], cell.shape)
+    def lift(cell, pick):
+        add = jnp.broadcast_to(pick(0), cell.shape)
         for m in range(1, COARSE):
-            add = jnp.where(cell == m, corr[m : m + 1], add)
+            add = jnp.where(cell == m, pick(m), add)
         return add
 
-    def whole(got, rsem):
-        pltpu.make_async_copy(got, got, rsem).wait()
-        return jnp.sum(got[...], axis=0)
-
-    south_k, own_k, north_k = corrections(inv_ref, gathered(msg_c, got_c, coarse_r.at[2]))
-    west_k = corrections(inv_w, whole(got_w, coarse_r.at[0]))
-    east_k = corrections(inv_e, whole(got_e, coarse_r.at[1]))
-    e = lift(cells, own_k)
-    eref = prs.at[2, 0]
-    eref[...] = e
-    near, far = split(
-        lift(mxlo[...], west_k[1]),
-        lift(mxhi[...], east_k[1]),
-        lift(mzlo[...], south_k),
-        lift(mzhi[...], north_k),
-    )
-    points = [
-        lift(mc[k], c) for k, c in enumerate((west_k[0], west_k[2], east_k[0], east_k[2]))
-    ]
-    edges = [
-        near[k] - face_share[k] * out
-        for k, out in enumerate(operate_faces(eref, near, far, points))
-    ]
-    e = e - share * operate(e, near)
-    e = e - share * operate(e, edges)
-    out_ref[...] = q + e
+    corr = [corrections(inv, restricted(t)) for inv, t in zip((inv_w, inv_ref, inv_e), (-1, 0, 1))]
+    half = lax.broadcasted_iota(jnp.int32, (8, ny), 0) < 4
+    spans = (pl.ds(0, 2), pl.ds(2, cx_n), pl.ds(cx_n + 2, 2))
+    raised = []
+    for k in range(3):
+        cell = cell_ref[spans[k]]
+        inside = lift(cell[:, :cz_n], lambda m: corr[k][1][m : m + 1])
+        outside = lift(
+            cell[:, cz_n:], lambda m: jnp.where(half, corr[k][2][m : m + 1], corr[k][0][m : m + 1])
+        )
+        raised.append(jnp.concatenate([inside, outside], 1))
+    e = jnp.concatenate(raised, 0)
+    e = e[1:-1] - shares(1) * smooth(e)
+    e = e[1:-1] - shares(0) * smooth(e)
+    out_ref[...] = (q + e)[:, :cz_n]
     for copy in pending:
         copy.wait_send()
 
@@ -564,21 +512,11 @@
     f32 = jnp.float32
     vmem = pltpu.VMEM
     dma = pltpu.SemaphoreType.DMA
+    n_spread = min(5, n_gx) * n_gz - 1
     n_sum = n_gx * n_gz - 1 if n_gx * n_gz <= DIRECT else n_gx - 1
 
     def block(fields, halo):
         return vmem((fields, cx_n + 2 * halo, deep, ny), f32)
-
-    def wide_set(kind):
-        return [
-            vmem((2 * cz_n, ny), kind),
-            vmem((2 * cz_n, ny), kind),
-            vmem((2, cx_n, ny), kind),
-            vmem((2, cx_n, ny), kind),
-            vmem((2, 2, cx_n, ny), kind),
-            vmem((4, 1, ny), kind),
-            vmem((4, 1, ny), kind),
-        ]
 
     scratch = [
         block(3, 2),
@@ -594,49 +532,37 @@
         block(3, 1),
         block(3, 1),
         block(3, 1),
-        vmem((5, 1, rows, ny), f32),
-        vmem((2, 1, cz_n, ny), f32),
-        vmem((2, 1, cz_n, ny), f32),
-        vmem((2, 1, cx_n, ny), f32),
-        vmem((2, 1, cx_n, ny), f32),
-        vmem((2, 2, 1, cx_n, ny), f32),
-        *wide_set(f32),
-        *wide_set(jnp.int32),
-        vmem((1, cz_n, ny), f32),
-        vmem((1, cz_n, ny), f32),
-        vmem((1, cx_n, ny), f32),
-        vmem((1, cx_n, ny), f32),
-        vmem((2, 1, cx_n, ny), f32),
+        vmem((cx_n + 4, deep, ny), jnp.int32),
+        vmem((cx_n + 4, deep, ny), jnp.int32),
+        vmem((cx_n + 4, deep, ny), f32),
+        vmem((cx_n + 4, deep, ny), f32),
+        vmem((cx_n + 6, deep, ny), f32),
         vmem(coarse_inverse.shape, f32),
         vmem(coarse_inverse.shape, f32),
         vmem((2, 1, 128), f32),
         vmem((2, n_sum, 1, 128), f32),
         vmem((2, 1, 128), f32),
         vmem((2, n_gz - 1, 1, 128), f32),
-        vmem((1, lanes), f32),
-        vmem((n_gz - 1, 1, lanes), f32),
-        vmem((n_gz, 1, lanes), f32),
-        vmem((n_gz, 1, lanes), f32),
-        dma((4, 4)),
-        dma((4, 4)),
-        dma((48,)),
-        dma((48,)),
+        vmem((3, 1, lanes), f32),
+        vmem((n_spread, 3, 1, lanes), f32),
+        dma((64,)),
+        dma((64,)),
         dma((2, n_sum)),
         dma((2,)),
         dma((2, n_gz - 1)),
         dma((2,)),
-        dma((3 * n_gz - 1,)),
-        dma((3,)),
+        dma((n_spread,)),
+        dma,
         dma((7,)),
-        dma((18,)),
-        dma((18,)),
+        dma((2,)),
+        dma((2,)),
     ]
     spec = pl.BlockSpec(memory_space=pltpu.VMEM)
     velocity, pressure = pl.pallas_call(
         functools.partial(kernel, (n_gx, n_gz, cx_n, cz_n, ny, lanes)),
         out_shape=(
             jax.ShapeDtypeStruct((3, cx_n, cz_n, ny), f32),
-            jax.ShapeDtypeStruct((rows, ny), f32),
+            jax.ShapeDtypeStruct((cx_n, cz_n, ny), f32),
         ),
         in_specs=[pl.BlockSpec(memory_space=pltpu.HBM)] * 7,
         out_specs=(spec, spec),
@@ -659,7 +585,7 @@
             )
         ]
     )
-    return velocity, pressure.reshape(cx_n, cz_n, ny)
+    return velocity, pressure
 
 
 def solution(mesh):

time: 38.8 us -> 36 us (0.928)
  Pallas kernels: 36.7 us -> 33.9 us
    pallas_call x1, Pallas kernels: 36.7 us -> 33.9 us  [body(): pl.pallas_call(functools.partial(kernel, (n_gx, n_gz, cx_n, cz_n, ny, lan...]
where the time goes in v1:
time: 36 us; the launch traced here: 35.9 us
  Pallas kernels  33.9 us (94%)
  local copies, waits for them, and re-layouts  1.31 us (4%)
  between operations  0.64 us (2%)
    pallas_call x1, Pallas kernels, body(): pl.pallas_call(functools.partial(kernel, (n_gx, n_gz, cx_n, cz_n, ny, lan...  33.9 us
    unnamed x2, local copies, waits for them, and re-layouts  1.31 us

profile of v1, /device:TPU:0, one launch (start us, length us, event | category | flops | bytes accessed | tf_op | source)
XLA Modules:
  0.0 35.9 jit_solution(15211482357932517722)
XLA Ops:
  0.6 33.9 %corrector.1 = (f32[3,8,16,128]{3,2,1,0:T(8,128)S(1)}, f32[8,16,128]{2,1,0:T(8,128)S(1)}) custom-call(f32[3,8,16,128]{3,2,1,0:T(8,128)} %x0_in.1, f32[3,8,16,128]{3,2,1,0:T(8,128)} %src_in.1, f32[8,16,128]{2,1,0:T(8,128)} %diag_in.1, f32[3,8,16,128]{3,2,1,0:T(8,128)} %face_in.1, s32[2,8,16]{2,1,0:T(8,128)} %bc_in.1, s32[128,128]{1,0:T(8,128)} %bitcast.1, ...), custom_call_target="tpu_custom_call" | custom-call | tf_op jit(solution)/shard_map/corrector/pallas_call | solution.py:561
  34.5 0.7 %copy.11 = f32[3,8,16,128]{3,2,1,0:T(8,128)} copy(f32[3,8,16,128]{3,2,1,0:T(8,128)S(1)} %get-tuple-element.4) | data formatting | bytes 393216
  35.2 0.6 %copy.12 = f32[8,16,128]{2,1,0:T(8,128)} copy(f32[8,16,128]{2,1,0:T(8,128)S(1)} %get-tuple-element.5) | data formatting | bytes 131072

commit v2 on v1

--- a/solution.py
+++ b/solution.py
@@ -259,6 +259,12 @@
     code = map_ref[...] + COARSE * flag
     code_ref[pl.ds(2, cx_n), pl.ds(0, cz_n)] = code.reshape(cx_n, cz_n, ny)
 
+    aside = to_corners(code_ref, code_ref, 2, 1)
+    aside += to_z(code_ref, code_ref, 2, 1, 2)
+    aside += to_x(code_ref, code_ref, 2, 1, 2)
+    aside.append(send(inv_ref, inv_w, side_s.at[0], side_r.at[0], east))
+    aside.append(send(inv_ref, inv_e, side_s.at[1], side_r.at[1], west))
+
     arrive(first)
     for x in range(cx_n + 4):
         cx, cx_low = face_ref[0, x + 1], face_ref[0, x]
@@ -285,6 +291,8 @@
     for to, sx, sz in zip(corners, (1, 1, -1, -1), (1, -1, 1, -1)):
         (fx, _), (fz, tz) = side_x(sx, 1, 1, 1), side_z(sz, 1, 1)
         second.append(ship(res_ref, r_far, to, (fx, fz), (side_x(sx, 2, 1, 1)[1], tz)))
+    zero = jnp.zeros((8, ny), jnp.float32)
+    sums_start(0, [p for d in dots for p in d + [(zero, zero)] * (PAD - 2)])
     second += to_z(vk_ref, vk_ref, 3, 1, 3)
     for sz in (1, -1):
         fz, tz = side_z(sz, 2, 2)
@@ -297,14 +305,6 @@
         fx, tx = side_x(sx, 1, 2, 2)[0], side_x(sx, 2, 2, 2)[1]
         z = pl.ds(0, cz_n)
         second.append(ship(res_ref, r_far, east if sx > 0 else west, (fx, z), (tx, z)))
-    zero = jnp.zeros((8, ny), jnp.float32)
-    sums_start(0, [p for d in dots for p in d + [(zero, zero)] * (PAD - 2)])
-
-    aside = to_corners(code_ref, code_ref, 2, 1)
-    aside += to_z(code_ref, code_ref, 2, 1, 2)
-    aside += to_x(code_ref, code_ref, 2, 1, 2)
-    aside.append(send(inv_ref, inv_w, side_s.at[0], side_r.at[0], east))
-    aside.append(send(inv_ref, inv_e, side_s.at[1], side_r.at[1], west))
 
     arrive(second)
     m0, m1 = sums_end(0, 2)

time: 36 us -> 35 us (0.972)
  Pallas kernels: 33.9 us -> 32.9 us
    pallas_call x1, Pallas kernels: 33.9 us -> 32.9 us  [body(): pl.pallas_call(functools.partial(kernel, (n_gx, n_gz, cx_n, cz_n, ny, lan...]
where the time goes in v2:
time: 35 us; the launch traced here: 34.9 us
  Pallas kernels  32.9 us (94%)
  local copies, waits for them, and re-layouts  1.31 us (4%)
  between operations  0.64 us (2%)
    pallas_call x1, Pallas kernels, body(): pl.pallas_call(functools.partial(kernel, (n_gx, n_gz, cx_n, cz_n, ny, lan...  32.9 us
    unnamed x2, local copies, waits for them, and re-layouts  1.31 us

profile of v2, /device:TPU:0, one launch (start us, length us, event | category | flops | bytes accessed | tf_op | source)
XLA Modules:
  0.0 34.9 jit_solution(17409963006585573246)
XLA Ops:
  0.6 32.9 %corrector.1 = (f32[3,8,16,128]{3,2,1,0:T(8,128)S(1)}, f32[8,16,128]{2,1,0:T(8,128)S(1)}) custom-call(f32[3,8,16,128]{3,2,1,0:T(8,128)} %x0_in.1, f32[3,8,16,128]{3,2,1,0:T(8,128)} %src_in.1, f32[8,16,128]{2,1,0:T(8,128)} %diag_in.1, f32[3,8,16,128]{3,2,1,0:T(8,128)} %face_in.1, s32[2,8,16]{2,1,0:T(8,128)} %bc_in.1, s32[128,128]{1,0:T(8,128)} %bitcast.1, ...), custom_call_target="tpu_custom_call" | custom-call | tf_op jit(solution)/shard_map/corrector/pallas_call | solution.py:561
  33.5 0.7 %copy.11 = f32[3,8,16,128]{3,2,1,0:T(8,128)} copy(f32[3,8,16,128]{3,2,1,0:T(8,128)S(1)} %get-tuple-element.4) | data formatting | bytes 393216
  34.2 0.6 %copy.12 = f32[8,16,128]{2,1,0:T(8,128)} copy(f32[8,16,128]{2,1,0:T(8,128)S(1)} %get-tuple-element.5) | data formatting | bytes 131072

commit v3 on v2

--- a/solution.py
+++ b/solution.py
@@ -20,7 +20,8 @@
     x0_in, src_in, diag_in, face_in, bc_in, map_in, inv_in,
     vel_ref, out_ref,
     x0_ref, src_ref, face_ref, bc_ref, map_ref, inv_ref,
-    coef, res_ref, r_far, vk_ref, a1_ref, a2_ref, a3_ref,
+    x0_late, src_late, face_late,
+    coef, res_ref, v_ref, vk_ref, a1_ref, a2_ref, a3_ref,
     code_ref, cell_ref, pd_ref, share_ref, q_ref, inv_w, inv_e,
     msg, got, msg_z, got_z, msg_c, got_c,
     near_s, near_r, sum_s, sum_r, sum_sz, sum_rz, coarse_s, coarse_r,
@@ -90,8 +91,8 @@
         pltpu.make_async_copy(a, b, load_sem.at[i])
         for i, (a, b) in enumerate(
             [
-                (x0_in, inner(x0_ref, 2)), (face_in, inner(face_ref.at[pl.ds(0, 3)], 3)),
-                (diag_in, inner(face_ref.at[3], 3)), (src_in, inner(src_ref, 1)),
+                (x0_in, inner(x0_ref, 3)), (face_in, inner(face_ref.at[pl.ds(0, 3)], 3)),
+                (diag_in, inner(face_ref.at[3], 3)), (src_in, inner(src_ref, 2)),
                 (bc_in, bc_ref), (map_in, map_ref), (inv_in, inv_ref),
             ]
         )
@@ -111,10 +112,10 @@
             return pl.ds(halo + cx_n - b, b - a + 1), pl.ds(halo - b, b - a + 1)
         return pl.ds(halo + a - 1, b - a + 1), pl.ds(halo + cx_n + a - 1, b - a + 1)
 
-    def side_z(sign, a, b):
+    def side_z(sign, a, b, base=0):
         if sign > 0:
-            return pl.ds(cz_n - b, b - a + 1), pl.ds(deep - b, b - a + 1)
-        return pl.ds(a - 1, b - a + 1), pl.ds(cz_n + a - 1, b - a + 1)
+            return pl.ds(cz_n - b, b - a + 1), pl.ds(deep - b - base, b - a + 1)
+        return pl.ds(a - 1, b - a + 1), pl.ds(cz_n + a - 1 - base, b - a + 1)
 
     used = []
 
@@ -126,17 +127,17 @@
             near_s.at[i], near_r.at[i], to,
         )
 
-    def to_corners(src, dst, halo, n):
+    def to_corners(src, dst, halo, n, base=0):
         out = []
         for to, sx, sz in zip(corners, (1, 1, -1, -1), (1, -1, 1, -1)):
-            (fx, tx), (fz, tz) = side_x(sx, halo, 1, n), side_z(sz, 1, n)
+            (fx, tx), (fz, tz) = side_x(sx, halo, 1, n), side_z(sz, 1, n, base)
             out.append(ship(src, dst, to, (fx, fz), (tx, tz)))
         return out
 
-    def to_z(src, dst, halo, a, b, ways=(1, -1)):
+    def to_z(src, dst, halo, a, b, ways=(1, -1), base=0):
         out = []
         for sz in ways:
-            fz, tz = side_z(sz, a, b)
+            fz, tz = side_z(sz, a, b, base)
             x = pl.ds(halo, cx_n)
             out.append(ship(src, dst, north if sz > 0 else south, (x, fz), (x, tz)))
         return out
@@ -149,16 +150,31 @@
             out.append(ship(src, dst, east if sx > 0 else west, (fx, z), (tx, z)))
         return out
 
-    first = to_corners(x0_ref, x0_ref, 2, 1)
-    first += to_corners(face_ref, face_ref, 3, 2)
-    first += to_z(x0_ref, x0_ref, 2, 1, 2)
-    first += to_z(face_ref, face_ref, 3, 1, 2)
-    first += to_z(face_ref.at[1], face_ref.at[1], 3, 3, 3, (1,))
-    first += to_z(src_ref, src_ref, 1, 1, 1)
-    first += to_x(x0_ref, x0_ref, 2, 1, 2)
-    first += to_x(face_ref, face_ref, 3, 1, 2)
-    first += to_x(face_ref.at[0], face_ref.at[0], 3, 3, 3, (1,))
-    first += to_x(src_ref, src_ref, 1, 1, 1)
+    both = pl.ds(0, 2)
+    first = to_corners(x0_ref, x0_ref, 3, 1)
+    first += to_corners(face_ref.at[both], face_ref.at[both], 3, 1)
+    first += to_z(x0_ref, x0_ref, 3, 1, 2)
+    first += to_z(face_ref, face_ref, 3, 1, 1)
+    first += to_z(face_ref.at[1], face_ref.at[1], 3, 2, 2, (1,))
+    first += to_z(src_ref, src_ref, 2, 1, 1)
+    first += to_x(x0_ref, x0_ref, 3, 1, 2)
+    first += to_x(face_ref, face_ref, 3, 1, 1)
+    first += to_x(face_ref.at[0], face_ref.at[0], 3, 2, 2, (1,))
+    first += to_x(src_ref, src_ref, 2, 1, 1)
+
+    rest = pl.ds(1, 3)
+    late = to_corners(x0_ref, x0_late, 3, 2, cz_n)
+    late += to_corners(face_ref, face_late, 3, 2, cz_n)
+    late += to_corners(src_ref, src_late, 2, 1, cz_n)
+    late += to_z(x0_ref, x0_late, 3, 3, 3, base=cz_n)
+    late += to_z(src_ref, src_late, 2, 2, 2, base=cz_n)
+    late += to_z(face_ref, face_late, 3, 2, 2, base=cz_n)
+    late += to_z(face_ref.at[1], face_late.at[1], 3, 3, 3, (1,), base=cz_n)
+    late += to_x(x0_ref, x0_ref, 3, 3, 3)
+    late += to_x(src_ref, src_ref, 2, 2, 2)
+    late += to_x(face_ref.at[rest], face_ref.at[rest], 3, 2, 2, (1,))
+    late += to_x(face_ref.at[0], face_ref.at[0], 3, 3, 3, (1,))
+    late += to_x(face_ref, face_ref, 3, 2, 2, (-1,))
 
     def arrive(copies):
         for copy in copies:
@@ -266,45 +282,63 @@
     aside.append(send(inv_ref, inv_e, side_s.at[1], side_r.at[1], west))
 
     arrive(first)
-    for x in range(cx_n + 4):
-        cx, cx_low = face_ref[0, x + 1], face_ref[0, x]
-        cz, cy = face_ref[1, x + 1], face_ref[2, x + 1]
-        cz_low = pltpu.roll(cz, 1, 0)
-        upper = jnp.where(lid, 0.0, cy)
-        lower = jnp.where(floor, 0.0, y_prev(cy))
-        wall = jnp.where(floor | lid, jnp.broadcast_to(cy[:, ny - 1 :], (deep, ny)), 0.0)
-        coef[0, x] = (face_ref[3, x + 1] + (cx + cz)) + ((upper + lower) + wall) + (cx_low + cz_low)
-        coef[1, x] = cz_low
-        coef[2, x] = upper
-        coef[3, x] = lower
-
+
+    def prepare(low, high):
+        for x in range(low, high):
+            cx, cx_low = face_ref[0, x + 1], face_ref[0, x]
+            cz, cy = face_ref[1, x + 1], face_ref[2, x + 1]
+            cz_low = pltpu.roll(cz, 1, 0)
+            upper = jnp.where(lid, 0.0, cy)
+            lower = jnp.where(floor, 0.0, y_prev(cy))
+            wall = jnp.where(floor | lid, jnp.broadcast_to(cy[:, ny - 1 :], (deep, ny)), 0.0)
+            total = (face_ref[3, x + 1] + (cx + cz)) + ((upper + lower) + wall)
+            coef[0, x] = total + (cx_low + cz_low)
+            coef[1, x] = cz_low
+            coef[2, x] = upper
+            coef[3, x] = lower
+
+    prepare(1, cx_n + 3)
     dots = []
     for c in range(3):
-        r = src_ref[c] - apply(x0_ref[c], c)
-        res_ref[c] = r
+        r = src_ref[c, pl.ds(1, cx_n + 2)] - apply(x0_ref[c, pl.ds(1, cx_n + 4)], c)
         r_own = own(r)
         v = apply(r, c)
         v_own = own(v)
         vk_ref[c, pl.ds(3, cx_n), pl.ds(0, cz_n)] = v[:, :cz_n]
         dots.append([(r_own, r_own), (r_own, v_own)])
     second = to_corners(vk_ref, vk_ref, 3, 2)
-    for to, sx, sz in zip(corners, (1, 1, -1, -1), (1, -1, 1, -1)):
-        (fx, _), (fz, tz) = side_x(sx, 1, 1, 1), side_z(sz, 1, 1)
-        second.append(ship(res_ref, r_far, to, (fx, fz), (side_x(sx, 2, 1, 1)[1], tz)))
     zero = jnp.zeros((8, ny), jnp.float32)
     sums_start(0, [p for d in dots for p in d + [(zero, zero)] * (PAD - 2)])
-    second += to_z(vk_ref, vk_ref, 3, 1, 3)
-    for sz in (1, -1):
-        fz, tz = side_z(sz, 2, 2)
-        second.append(
-            ship(res_ref, r_far, north if sz > 0 else south,
-                 (pl.ds(1, cx_n), fz), (pl.ds(2, cx_n), tz))
-        )
-    second += to_x(vk_ref, vk_ref, 3, 1, 3)
-    for sx in (1, -1):
-        fx, tx = side_x(sx, 1, 2, 2)[0], side_x(sx, 2, 2, 2)[1]
-        z = pl.ds(0, cz_n)
-        second.append(ship(res_ref, r_far, east if sx > 0 else west, (fx, z), (tx, z)))
+    second += to_z(vk_ref, vk_ref, 3, 2, 3)
+    second += to_x(vk_ref, vk_ref, 3, 2, 3)
+
+    arrive(late)
+    beyond = pl.ds(cz_n, 8)
+    nearest = (slot[cz_n:] == cz_n) | (slot[cz_n:] == deep - 1)
+    farthest = (slot[cz_n:] == cz_n + 2) | (slot[cz_n:] == deep - 3)
+    middle = pl.ds(3, cx_n)
+    for f in range(4):
+        face_ref[f, middle, beyond] = jnp.where(
+            nearest, face_ref[f, middle, beyond], face_late[f, middle]
+        )
+        for x in (1, cx_n + 3):
+            face_ref[f, pl.ds(x, 2), beyond] = face_late[f, pl.ds(x, 2)]
+    prepare(0, cx_n + 4)
+    inside = pl.ds(2, cx_n)
+    for c in range(3):
+        x0_ref[c, middle, beyond] = jnp.where(
+            farthest, x0_late[c, middle], x0_ref[c, middle, beyond]
+        )
+        for x in (1, cx_n + 3):
+            x0_ref[c, pl.ds(x, 2), beyond] = x0_late[c, pl.ds(x, 2)]
+        src_ref[c, inside, beyond] = jnp.where(
+            nearest, src_ref[c, inside, beyond], src_late[c, inside]
+        )
+        for x in (1, cx_n + 2):
+            src_ref[c, x, beyond] = src_late[c, x]
+        r = src_ref[c] - apply(x0_ref[c], c)
+        res_ref[c] = r
+        v_ref[c] = apply(r, c)
 
     arrive(second)
     m0, m1 = sums_end(0, 2)
@@ -314,13 +348,13 @@
     dots = []
     for c in range(3):
         s = sigma[c : c + 1]
-        v = vk_ref[c]
-        mid_r = jnp.where(mine, res_ref[c, pl.ds(1, cx_n)], r_far[c, pl.ds(2, cx_n)])
-        lo_r = jnp.where(body_rows, res_ref[c, 0], r_far[c, 1])
-        hi_r = jnp.where(body_rows, res_ref[c, cx_n + 1], r_far[c, cx_n + 2])
-        r = jnp.concatenate(
-            [r_far[c, pl.ds(0, 1)], lo_r[None], mid_r, hi_r[None], r_far[c, pl.ds(cx_n + 3, 1)]], 0
-        )
+        mid = jnp.where(mine, v_ref[c, pl.ds(1, cx_n)], vk_ref[c, pl.ds(3, cx_n)])
+        low = jnp.where(body_rows, v_ref[c, 0], vk_ref[c, 2])
+        high = jnp.where(body_rows, v_ref[c, cx_n + 1], vk_ref[c, cx_n + 3])
+        v = jnp.concatenate(
+            [vk_ref[c, pl.ds(0, 2)], low[None], mid, high[None], vk_ref[c, pl.ds(cx_n + 4, 2)]], 0
+        )
+        r = res_ref[c]
         u = apply(v, c)
         v = v[1:-1]
         a1 = v - s * r
@@ -383,7 +417,7 @@
     speed = []
     for c in range(3):
         w = [k[c : c + 1] for k in weight]
-        field = x0_ref[c, pl.ds(1, cx_n + 2)] + w[0] * res_ref[c]
+        field = x0_ref[c, pl.ds(2, cx_n + 2)] + w[0] * res_ref[c, pl.ds(1, cx_n + 2)]
         field += w[1] * a1_ref[c] + w[2] * a2_ref[c] + w[3] * a3_ref[c]
         vel_ref[c] = field[1:-1, :cz_n]
         speed.append(field)
@@ -503,6 +537,16 @@
         copy.wait_send()
 
 
+def put(a_ref, b_ref, a_out, b_out, sem):
+    copies = [
+        pltpu.make_async_copy(a_ref, a_out, sem.at[0]), pltpu.make_async_copy(b_ref, b_out, sem.at[1])
+    ]
+    for copy in copies:
+        copy.start()
+    for copy in copies:
+        copy.wait()
+
+
 def body(n_gx, n_gz, velocity_old, source, diag_coef, face_coef, bc_flags, coarse_map, coarse_inverse):
     cx_n, cz_n, ny = diag_coef.shape
     rows = cx_n * cz_n
@@ -519,15 +563,18 @@
         return vmem((fields, cx_n + 2 * halo, deep, ny), f32)
 
     scratch = [
+        block(3, 3),
         block(3, 2),
-        block(3, 1),
         block(4, 3),
         vmem(bc_flags.shape, jnp.int32),
         vmem((rows, ny), jnp.int32),
         vmem(coarse_inverse.shape, f32),
+        vmem((3, cx_n + 6, 8, ny), f32),
+        vmem((3, cx_n + 4, 8, ny), f32),
+        vmem((4, cx_n + 6, 8, ny), f32),
         block(4, 2),
+        block(3, 2),
         block(3, 1),
-        block(3, 2),
         block(3, 3),
         block(3, 1),
         block(3, 1),
@@ -545,8 +592,8 @@
         vmem((2, n_gz - 1, 1, 128), f32),
         vmem((3, 1, lanes), f32),
         vmem((n_spread, 3, 1, lanes), f32),
-        dma((64,)),
-        dma((64,)),
+        dma((96,)),
+        dma((96,)),
         dma((2, n_sum)),
         dma((2,)),
         dma((2, n_gz - 1)),
@@ -585,6 +632,17 @@
             )
         ]
     )
+    velocity, pressure = pl.pallas_call(
+        put,
+        out_shape=(
+            jax.ShapeDtypeStruct(velocity.shape, f32),
+            jax.ShapeDtypeStruct(pressure.shape, f32),
+        ),
+        in_specs=[spec, spec],
+        out_specs=[pl.BlockSpec(memory_space=pltpu.HBM)] * 2,
+        scratch_shapes=[dma((2,))],
+        name="put",
+    )(*[pltpu.with_memory_space_constraint(a, pltpu.VMEM) for a in (velocity, pressure)])
     return velocity, pressure
 
 

time: 35 us -> 33 us (0.943)
  local copies, waits for them, and re-layouts: 1.31 us -> 0 us
  Pallas kernels: 32.9 us -> 32.3 us
    pallas_call x1, Pallas kernels: 32.9 us -> 31.5 us  [body(): pl.pallas_call(functools.partial(kernel, (n_gx, n_gz, cx_n, cz_n, ny, lan...]
    unnamed x2 -> x0, local copies, waits for them, and re-layouts: 1.31 us -> none
    pallas_call x0 -> x1, Pallas kernels: none -> 0.71 us  [body(): pl.pallas_call(put, out_shape=(jax.ShapeDtypeStruct(velocity.shape, f32),...]
where the time goes in v3:
time: 33 us; the launch traced here: 32.9 us
  Pallas kernels  32.3 us (98%)
  between operations  0.64 us (2%)
    pallas_call x1, Pallas kernels, body(): pl.pallas_call(functools.partial(kernel, (n_gx, n_gz, cx_n, cz_n, ny, lan...  31.5 us
    pallas_call x1, Pallas kernels, body(): pl.pallas_call(put, out_shape=(jax.ShapeDtypeStruct(velocity.shape, f32),...  0.71 us

profile of v3, /device:TPU:0, one launch (start us, length us, event | category | flops | bytes accessed | tf_op | source)
XLA Modules:
  0.0 32.9 jit_solution(14571137298557291323)
XLA Ops:
  0.6 31.5 %corrector.1 = (f32[3,8,16,128]{3,2,1,0:T(8,128)S(1)}, f32[8,16,128]{2,1,0:T(8,128)S(1)}) custom-call(f32[3,8,16,128]{3,2,1,0:T(8,128)} %x0_in.1, f32[3,8,16,128]{3,2,1,0:T(8,128)} %src_in.1, f32[8,16,128]{2,1,0:T(8,128)} %diag_in.1, f32[3,8,16,128]{3,2,1,0:T(8,128)} %face_in.1, s32[2,8,16]{2,1,0:T(8,128)} %bc_in.1, s32[128,128]{1,0:T(8,128)} %bitcast.1, ...), custom_call_target="tpu_custom_call" | custom-call | tf_op jit(solution)/shard_map/corrector/pallas_call | solution.py:608
  32.2 0.7 %put.1 = (f32[3,8,16,128]{3,2,1,0:T(8,128)}, f32[8,16,128]{2,1,0:T(8,128)}) custom-call(f32[3,8,16,128]{3,2,1,0:T(8,128)S(1)} %get-tuple-element.4.a_ref, f32[8,16,128]{2,1,0:T(8,128)S(1)} %get-tuple-element.5.b_ref), custom_call_target="tpu_custom_call" | custom-call | tf_op jit(solution)/shard_map/put/pallas_call | solution.py:635

commit v4 on v3

--- a/solution.py
+++ b/solution.py
@@ -1,4 +1,5 @@
 import functools
+import math
 
 import jax
 import jax.numpy as jnp
@@ -24,8 +25,7 @@
     coef, res_ref, v_ref, vk_ref, a1_ref, a2_ref, a3_ref,
     code_ref, cell_ref, pd_ref, share_ref, q_ref, inv_w, inv_e,
     msg, got, msg_z, got_z, msg_c, got_c,
-    near_s, near_r, sum_s, sum_r, sum_sz, sum_rz, coarse_s, coarse_r,
-    load_sem, side_s, side_r,
+    tally, near_s, near_r, sum_sem, coarse_sem, load_sem, side_s, side_r,
 ):
     n_gx, n_gz, cx_n, cz_n, ny, lanes = dims
     rows = cx_n * cz_n
@@ -39,7 +39,6 @@
     row_x = [(lax.rem(gx + d, n_gx), gz) for d in range(1, n_gx)]
     row_z = [(gx, lax.rem(gz + d, n_gz)) for d in range(1, n_gz)]
     direct = n_gx * n_gz <= DIRECT
-    pending = []
 
     def send(src, dst, ssem, rsem, to):
         copy = pltpu.make_async_remote_copy(
@@ -47,8 +46,11 @@
             device_id=to, device_id_type=MESH,
         )
         copy.start()
-        pending.append(copy)
         return copy
+
+    def settle(sem, count):
+        span = tally.at[pl.ds(0, count)]
+        pltpu.make_async_copy(span, span, sem).wait()
 
     corners = [
         (east[0], north[1]), (east[0], south[1]), (west[0], north[1]), (west[0], south[1])
@@ -82,13 +84,14 @@
         sum_to = row_x
         met = around | set(spread_to)
         met |= {(d, 0) for d in range(1, n_gx)} | {(0, k) for k in range(1, n_gz)}
-    partners = [at(o) for o in sorted(around)] + [at(o) for o in sorted(met - around)]
+    near_first = sorted(around, key=lambda o: (o[0] == 0) + (o[1] == 0) * 2)
+    partners = [at(o) for o in near_first] + [at(o) for o in sorted(met - around)]
 
     def inner(ref, halo):
         return ref.at[..., pl.ds(halo, cx_n), pl.ds(0, cz_n), :]
 
     loads = [
-        pltpu.make_async_copy(a, b, load_sem.at[i])
+        pltpu.make_async_copy(a, b, load_sem.at[max(0, i - 3)])
         for i, (a, b) in enumerate(
             [
                 (x0_in, inner(x0_ref, 3)), (face_in, inner(face_ref.at[pl.ds(0, 3)], 3)),
@@ -97,13 +100,12 @@
             ]
         )
     ]
-    for load in loads:
-        load.start()
     barrier = pltpu.get_barrier_semaphore()
     for other in partners:
         pl.semaphore_signal(barrier, inc=1, device_id=other, device_id_type=MESH)
-    for load in loads[:4]:
-        load.wait()
+    for load in loads:
+        load.start()
+    settle(load_sem.at[0], 10 * rows)
     pl.semaphore_wait(barrier, len(partners))
 
 
@@ -117,68 +119,61 @@
             return pl.ds(cz_n - b, b - a + 1), pl.ds(deep - b - base, b - a + 1)
         return pl.ds(a - 1, b - a + 1), pl.ds(cz_n + a - 1 - base, b - a + 1)
 
-    used = []
+    lots = []
 
     def ship(src, dst, to, where_from, where_to):
-        i = len(used)
-        used.append(i)
-        return send(
-            src.at[(..., *where_from, slice(None))], dst.at[(..., *where_to, slice(None))],
-            near_s.at[i], near_r.at[i], to,
-        )
+        target = dst.at[(..., *where_to, slice(None))]
+        lots[-1] += math.prod(target.shape[:-1])
+        i = len(lots) - 1
+        send(src.at[(..., *where_from, slice(None))], target, near_s.at[i], near_r.at[i], to)
+
+    def arrive(i):
+        settle(near_r.at[i], lots[i])
 
     def to_corners(src, dst, halo, n, base=0):
-        out = []
         for to, sx, sz in zip(corners, (1, 1, -1, -1), (1, -1, 1, -1)):
             (fx, tx), (fz, tz) = side_x(sx, halo, 1, n), side_z(sz, 1, n, base)
-            out.append(ship(src, dst, to, (fx, fz), (tx, tz)))
-        return out
+            ship(src, dst, to, (fx, fz), (tx, tz))
 
     def to_z(src, dst, halo, a, b, ways=(1, -1), base=0):
-        out = []
         for sz in ways:
             fz, tz = side_z(sz, a, b, base)
             x = pl.ds(halo, cx_n)
-            out.append(ship(src, dst, north if sz > 0 else south, (x, fz), (x, tz)))
-        return out
+            ship(src, dst, north if sz > 0 else south, (x, fz), (x, tz))
 
     def to_x(src, dst, halo, a, b, ways=(1, -1)):
-        out = []
         for sx in ways:
             fx, tx = side_x(sx, halo, a, b)
             z = pl.ds(0, cz_n)
-            out.append(ship(src, dst, east if sx > 0 else west, (fx, z), (tx, z)))
-        return out
+            ship(src, dst, east if sx > 0 else west, (fx, z), (tx, z))
 
     both = pl.ds(0, 2)
-    first = to_corners(x0_ref, x0_ref, 3, 1)
-    first += to_corners(face_ref.at[both], face_ref.at[both], 3, 1)
-    first += to_z(x0_ref, x0_ref, 3, 1, 2)
-    first += to_z(face_ref, face_ref, 3, 1, 1)
-    first += to_z(face_ref.at[1], face_ref.at[1], 3, 2, 2, (1,))
-    first += to_z(src_ref, src_ref, 2, 1, 1)
-    first += to_x(x0_ref, x0_ref, 3, 1, 2)
-    first += to_x(face_ref, face_ref, 3, 1, 1)
-    first += to_x(face_ref.at[0], face_ref.at[0], 3, 2, 2, (1,))
-    first += to_x(src_ref, src_ref, 2, 1, 1)
+    lots.append(0)
+    to_corners(x0_ref, x0_ref, 3, 1)
+    to_corners(face_ref.at[both], face_ref.at[both], 3, 1)
+    to_z(x0_ref, x0_ref, 3, 1, 2)
+    to_z(face_ref, face_ref, 3, 1, 1)
+    to_z(face_ref.at[1], face_ref.at[1], 3, 2, 2, (1,))
+    to_z(src_ref, src_ref, 2, 1, 1)
+    to_x(x0_ref, x0_ref, 3, 1, 2)
+    to_x(face_ref, face_ref, 3, 1, 1)
+    to_x(face_ref.at[0], face_ref.at[0], 3, 2, 2, (1,))
+    to_x(src_ref, src_ref, 2, 1, 1)
 
     rest = pl.ds(1, 3)
-    late = to_corners(x0_ref, x0_late, 3, 2, cz_n)
-    late += to_corners(face_ref, face_late, 3, 2, cz_n)
-    late += to_corners(src_ref, src_late, 2, 1, cz_n)
-    late += to_z(x0_ref, x0_late, 3, 3, 3, base=cz_n)
-    late += to_z(src_ref, src_late, 2, 2, 2, base=cz_n)
-    late += to_z(face_ref, face_late, 3, 2, 2, base=cz_n)
-    late += to_z(face_ref.at[1], face_late.at[1], 3, 3, 3, (1,), base=cz_n)
-    late += to_x(x0_ref, x0_ref, 3, 3, 3)
-    late += to_x(src_ref, src_ref, 2, 2, 2)
-    late += to_x(face_ref.at[rest], face_ref.at[rest], 3, 2, 2, (1,))
-    late += to_x(face_ref.at[0], face_ref.at[0], 3, 3, 3, (1,))
-    late += to_x(face_ref, face_ref, 3, 2, 2, (-1,))
-
-    def arrive(copies):
-        for copy in copies:
-            copy.wait_recv()
+    lots.append(0)
+    to_corners(x0_ref, x0_late, 3, 2, cz_n)
+    to_corners(face_ref, face_late, 3, 2, cz_n)
+    to_corners(src_ref, src_late, 2, 1, cz_n)
+    to_z(x0_ref, x0_late, 3, 3, 3, base=cz_n)
+    to_z(src_ref, src_late, 2, 2, 2, base=cz_n)
+    to_z(face_ref, face_late, 3, 2, 2, base=cz_n)
+    to_z(face_ref.at[1], face_late.at[1], 3, 3, 3, (1,), base=cz_n)
+    to_x(x0_ref, x0_ref, 3, 3, 3)
+    to_x(src_ref, src_ref, 2, 2, 2)
+    to_x(face_ref.at[rest], face_ref.at[rest], 3, 2, 2, (1,))
+    to_x(face_ref.at[0], face_ref.at[0], 3, 3, 3, (1,))
+    to_x(face_ref, face_ref, 3, 2, 2, (-1,))
 
     level = lax.broadcasted_iota(jnp.int32, (rows, ny), 1)
     bottom = level == 0
@@ -204,29 +199,28 @@
         ]
         return jnp.broadcast_to(jnp.concatenate(parts, 0), (rows, ny))
 
-    def scatter(msg, got, ssem, rsem, others):
-        return [
-            send(msg, got.at[d], ssem.at[d], rsem, to) for d, to in enumerate(others)
-        ]
-
-    def gathered(msg, got, rsem):
-        pltpu.make_async_copy(got, got, rsem).wait()
+    def scatter(msg, got, sem, others):
+        for d, to in enumerate(others):
+            send(msg, got.at[d], sem.at[0], sem.at[1], to)
+
+    def gathered(msg, got, sem):
+        for k in range(2):
+            pltpu.make_async_copy(got, got, sem.at[k]).wait()
         return msg[...] + jnp.sum(got[...], axis=0)
-
 
     def z_roll(f, shift):
         flat = f.reshape((-1,) + f.shape[-2:])
         return pltpu.roll(flat, shift % deep, 1).reshape(f.shape)
 
-    def apply(f, c):
+    def apply(f):
         h = (f.shape[0] - cx_n) // 2 - 1
         n = cx_n + 2 * h
         g = f[1:-1]
-        total = coef[0, pl.ds(2 - h, n)] * g
-        total -= face_ref[0, pl.ds(3 - h, n)] * f[2:] + face_ref[0, pl.ds(2 - h, n)] * f[:-2]
-        total -= face_ref[1, pl.ds(3 - h, n)] * z_roll(g, -1) + coef[1, pl.ds(2 - h, n)] * z_roll(g, 1)
-        total -= coef[2, pl.ds(2 - h, n)] * y_next(g) + coef[3, pl.ds(2 - h, n)] * y_prev(g)
-        return total
+        flux_x = face_ref[0, pl.ds(2 - h, n + 1)] * (f[:-1] - f[1:])
+        flux_z = face_ref[1, pl.ds(3 - h, n)] * (g - z_roll(g, -1))
+        flux_y = coef[1, pl.ds(2 - h, n)] * (g - y_next(g))
+        total = coef[0, pl.ds(2 - h, n)] * g + (flux_x[1:] - flux_x[:-1])
+        return total + (flux_z - z_roll(flux_z, 1)) + (flux_y - y_prev(flux_y))
 
     def own(f):
         h = (f.shape[0] - cx_n) // 2
@@ -247,14 +241,14 @@
 
     def sums_start(i, pairs):
         msg[i] = pack(pairs)
-        scatter(msg.at[i], got.at[i], sum_s.at[i], sum_r.at[i], sum_to)
+        scatter(msg.at[i], got.at[i], sum_sem.at[i, 0], sum_to)
 
     def sums_end(i, count):
-        total = gathered(msg.at[i], got.at[i], sum_r.at[i])
+        total = gathered(msg.at[i], got.at[i], sum_sem.at[i, 0])
         if not direct:
             msg_z[i] = total
-            scatter(msg_z.at[i], got_z.at[i], sum_sz.at[i], sum_rz.at[i], row_z)
-            total = gathered(msg_z.at[i], got_z.at[i], sum_rz.at[i])
+            scatter(msg_z.at[i], got_z.at[i], sum_sem.at[i, 1], row_z)
+            total = gathered(msg_z.at[i], got_z.at[i], sum_sem.at[i, 1])
         shape = (8, 128)
         place = lax.broadcasted_iota(jnp.int32, shape, 0) * PAD
         lane = lax.broadcasted_iota(jnp.int32, shape, 1)
@@ -275,44 +269,41 @@
     code = map_ref[...] + COARSE * flag
     code_ref[pl.ds(2, cx_n), pl.ds(0, cz_n)] = code.reshape(cx_n, cz_n, ny)
 
-    aside = to_corners(code_ref, code_ref, 2, 1)
-    aside += to_z(code_ref, code_ref, 2, 1, 2)
-    aside += to_x(code_ref, code_ref, 2, 1, 2)
-    aside.append(send(inv_ref, inv_w, side_s.at[0], side_r.at[0], east))
-    aside.append(send(inv_ref, inv_e, side_s.at[1], side_r.at[1], west))
-
-    arrive(first)
+    lots.append(0)
+    to_corners(code_ref, code_ref, 2, 1)
+    to_z(code_ref, code_ref, 2, 1, 2)
+    to_x(code_ref, code_ref, 2, 1, 2)
+    blocks = [
+        send(inv_ref, inv_w, side_s.at[0], side_r.at[0], east),
+        send(inv_ref, inv_e, side_s.at[1], side_r.at[1], west),
+    ]
+
+    arrive(0)
 
     def prepare(low, high):
         for x in range(low, high):
-            cx, cx_low = face_ref[0, x + 1], face_ref[0, x]
-            cz, cy = face_ref[1, x + 1], face_ref[2, x + 1]
-            cz_low = pltpu.roll(cz, 1, 0)
-            upper = jnp.where(lid, 0.0, cy)
-            lower = jnp.where(floor, 0.0, y_prev(cy))
+            cy = face_ref[2, x + 1]
             wall = jnp.where(floor | lid, jnp.broadcast_to(cy[:, ny - 1 :], (deep, ny)), 0.0)
-            total = (face_ref[3, x + 1] + (cx + cz)) + ((upper + lower) + wall)
-            coef[0, x] = total + (cx_low + cz_low)
-            coef[1, x] = cz_low
-            coef[2, x] = upper
-            coef[3, x] = lower
+            coef[0, x] = face_ref[3, x + 1] + wall
+            coef[1, x] = jnp.where(lid, 0.0, cy)
 
     prepare(1, cx_n + 3)
     dots = []
     for c in range(3):
-        r = src_ref[c, pl.ds(1, cx_n + 2)] - apply(x0_ref[c, pl.ds(1, cx_n + 4)], c)
+        r = src_ref[c, pl.ds(1, cx_n + 2)] - apply(x0_ref[c, pl.ds(1, cx_n + 4)])
         r_own = own(r)
-        v = apply(r, c)
+        v = apply(r)
         v_own = own(v)
         vk_ref[c, pl.ds(3, cx_n), pl.ds(0, cz_n)] = v[:, :cz_n]
         dots.append([(r_own, r_own), (r_own, v_own)])
-    second = to_corners(vk_ref, vk_ref, 3, 2)
+    lots.append(0)
+    to_corners(vk_ref, vk_ref, 3, 2)
     zero = jnp.zeros((8, ny), jnp.float32)
     sums_start(0, [p for d in dots for p in d + [(zero, zero)] * (PAD - 2)])
-    second += to_z(vk_ref, vk_ref, 3, 2, 3)
-    second += to_x(vk_ref, vk_ref, 3, 2, 3)
-
-    arrive(late)
+    to_z(vk_ref, vk_ref, 3, 2, 3)
+    to_x(vk_ref, vk_ref, 3, 2, 3)
+
+    arrive(1)
     beyond = pl.ds(cz_n, 8)
     nearest = (slot[cz_n:] == cz_n) | (slot[cz_n:] == deep - 1)
     farthest = (slot[cz_n:] == cz_n + 2) | (slot[cz_n:] == deep - 3)
@@ -336,11 +327,11 @@
         )
         for x in (1, cx_n + 2):
             src_ref[c, x, beyond] = src_late[c, x]
-        r = src_ref[c] - apply(x0_ref[c], c)
+        r = src_ref[c] - apply(x0_ref[c])
         res_ref[c] = r
-        v_ref[c] = apply(r, c)
-
-    arrive(second)
+        v_ref[c] = apply(r)
+
+    arrive(3)
     m0, m1 = sums_end(0, 2)
     sigma = m1 / m0
     mine = (slot <= cz_n) | (slot == deep - 1)
@@ -355,12 +346,12 @@
             [vk_ref[c, pl.ds(0, 2)], low[None], mid, high[None], vk_ref[c, pl.ds(cx_n + 4, 2)]], 0
         )
         r = res_ref[c]
-        u = apply(v, c)
+        u = apply(v)
         v = v[1:-1]
         a1 = v - s * r
         a2 = (u - s * v) - s * a1
-        a3 = apply(a2, c) - s * a2[1:-1]
-        a4 = apply(a3, c) - s * a3[1:-1]
+        a3 = apply(a2) - s * a2[1:-1]
+        a4 = apply(a3) - s * a3[1:-1]
         r0, b1, b2, b3, b4 = own(r), own(a1), own(a2), own(a3), own(a4)
         dots += [
             (r0, b1), (b1, b1), (b1, b2), (b2, b2), (b2, b3), (b3, b3), (b3, b4), (b4, b4)
@@ -369,7 +360,9 @@
         a2_ref[c] = a2[1:-1]
         a3_ref[c] = a3
     sums_start(1, dots)
-    arrive(aside)
+    arrive(2)
+    for block in blocks:
+        block.wait()
     for x in range(cx_n + 4):
         mark = code_ref[x] >= COARSE
         edge = floor | lid
@@ -428,9 +421,10 @@
     share = share_ref[pl.ds(2, cx_n)]
     q = share * div
     q_ref[pl.ds(3, cx_n), pl.ds(0, cz_n)] = q[:, :cz_n]
-    third = to_corners(q_ref, q_ref, 3, 2)
-    third += to_z(q_ref, q_ref, 3, 1, 3)
-    third += to_x(q_ref, q_ref, 3, 1, 3)
+    lots.append(0)
+    to_corners(q_ref, q_ref, 3, 2)
+    to_z(q_ref, q_ref, 3, 1, 3)
+    to_x(q_ref, q_ref, 3, 1, 3)
 
     def smooth(f):
         n = f.shape[0] - 2
@@ -487,15 +481,19 @@
             for place, col in zip(places, cols)
         )
         msg_c[k] = jnp.sum(line, axis=0, keepdims=True)
-    scatter(msg_c, got_c, coarse_s, coarse_r, [at(o) for o in spread_to])
-
-    arrive(third)
+    scatter(msg_c, got_c, coarse_sem, [at(o) for o in spread_to])
+
+    for i in range(4):
+        settle(near_s.at[i], lots[i])
+    arrive(4)
     ext = q_ref[...]
     q = 2.0 * ext[1:-1] - shares(2) * smooth(ext)
     q = q[1:-1] + ext[2:-2] - shares(1) * smooth(q)
     q = q[1:-1] + ext[3:-3] - shares(0) * smooth(q)
 
-    pltpu.make_async_copy(got_c, got_c, coarse_r).wait()
+    settle(near_s.at[4], lots[4])
+    for k in range(2):
+        pltpu.make_async_copy(got_c, got_c, coarse_sem.at[k]).wait()
 
     def restricted(t):
         rows_in = [
@@ -533,8 +531,6 @@
     e = e[1:-1] - shares(1) * smooth(e)
     e = e[1:-1] - shares(0) * smooth(e)
     out_ref[...] = (q + e)[:, :cz_n]
-    for copy in pending:
-        copy.wait_send()
 
 
 def put(a_ref, b_ref, a_out, b_out, sem):
@@ -572,7 +568,7 @@
         vmem((3, cx_n + 6, 8, ny), f32),
         vmem((3, cx_n + 4, 8, ny), f32),
         vmem((4, cx_n + 6, 8, ny), f32),
-        block(4, 2),
+        block(2, 2),
         block(3, 2),
         block(3, 1),
         block(3, 3),
@@ -592,15 +588,12 @@
         vmem((2, n_gz - 1, 1, 128), f32),
         vmem((3, 1, lanes), f32),
         vmem((n_spread, 3, 1, lanes), f32),
-        dma((96,)),
-        dma((96,)),
-        dma((2, n_sum)),
+        vmem((2048, ny), f32),
+        dma((5,)),
+        dma((5,)),
+        dma((2, 2, 2) if n_sum < n_gx * n_gz - 1 else (2, 1, 2)),
         dma((2,)),
-        dma((2, n_gz - 1)),
-        dma((2,)),
-        dma((n_spread,)),
-        dma,
-        dma((7,)),
+        dma((4,)),
         dma((2,)),
         dma((2,)),
     ]

time: 33 us -> 30.5 us (0.924)
  Pallas kernels: 32.3 us -> 29.7 us
    pallas_call x1, Pallas kernels: 31.5 us -> 29 us  [body(): pl.pallas_call(functools.partial(kernel, (n_gx, n_gz, cx_n, cz_n, ny, lan...]
where the time goes in v4:
time: 30.5 us; the launch traced here: 30.3 us
  Pallas kernels  29.7 us (97%)
  between operations  0.64 us (2%)
    pallas_call x1, Pallas kernels, body(): pl.pallas_call(functools.partial(kernel, (n_gx, n_gz, cx_n, cz_n, ny, lan...  29 us
    pallas_call x1, Pallas kernels, body(): pl.pallas_call(put, out_shape=(jax.ShapeDtypeStruct(velocity.shape, f32),...  0.71 us

profile of v4, /device:TPU:0, one launch (start us, length us, event | category | flops | bytes accessed | tf_op | source)
XLA Modules:
  0.0 30.3 jit_solution(8482344738695651125)
XLA Ops:
  0.6 29.0 %corrector.1 = (f32[3,8,16,128]{3,2,1,0:T(8,128)S(1)}, f32[8,16,128]{2,1,0:T(8,128)S(1)}) custom-call(f32[3,8,16,128]{3,2,1,0:T(8,128)} %x0_in.1, f32[3,8,16,128]{3,2,1,0:T(8,128)} %src_in.1, f32[8,16,128]{2,1,0:T(8,128)} %diag_in.1, f32[3,8,16,128]{3,2,1,0:T(8,128)} %face_in.1, s32[2,8,16]{2,1,0:T(8,128)} %bc_in.1, s32[128,128]{1,0:T(8,128)} %bitcast.1, ...), custom_call_target="tpu_custom_call" | custom-call | tf_op jit(solution)/shard_map/corrector/pallas_call | solution.py:601
  29.6 0.7 %put.1 = (f32[3,8,16,128]{3,2,1,0:T(8,128)}, f32[8,16,128]{2,1,0:T(8,128)}) custom-call(f32[3,8,16,128]{3,2,1,0:T(8,128)S(1)} %get-tuple-element.4.a_ref, f32[8,16,128]{2,1,0:T(8,128)S(1)} %get-tuple-element.5.b_ref), custom_call_target="tpu_custom_call" | custom-call | tf_op jit(solution)/shard_map/put/pallas_call | solution.py:628

commit v5 on v4

--- a/solution.py
+++ b/solution.py
@@ -21,7 +21,7 @@
     x0_in, src_in, diag_in, face_in, bc_in, map_in, inv_in,
     vel_ref, out_ref,
     x0_ref, src_ref, face_ref, bc_ref, map_ref, inv_ref,
-    x0_late, src_late, face_late,
+    x0_late, rho_ref, rho_late, edge_ref,
     coef, res_ref, v_ref, vk_ref, a1_ref, a2_ref, a3_ref,
     code_ref, cell_ref, pd_ref, share_ref, q_ref, inv_w, inv_e,
     msg, got, msg_z, got_z, msg_c, got_c,
@@ -94,8 +94,8 @@
         pltpu.make_async_copy(a, b, load_sem.at[max(0, i - 3)])
         for i, (a, b) in enumerate(
             [
-                (x0_in, inner(x0_ref, 3)), (face_in, inner(face_ref.at[pl.ds(0, 3)], 3)),
-                (diag_in, inner(face_ref.at[3], 3)), (src_in, inner(src_ref, 2)),
+                (x0_in, inner(x0_ref, 2)), (face_in, inner(face_ref.at[pl.ds(0, 3)], 3)),
+                (diag_in, inner(face_ref.at[3], 3)), (src_in, src_ref),
                 (bc_in, bc_ref), (map_in, map_ref), (inv_in, inv_ref),
             ]
         )
@@ -114,10 +114,10 @@
             return pl.ds(halo + cx_n - b, b - a + 1), pl.ds(halo - b, b - a + 1)
         return pl.ds(halo + a - 1, b - a + 1), pl.ds(halo + cx_n + a - 1, b - a + 1)
 
-    def side_z(sign, a, b, base=0):
+    def side_z(sign, a, b):
         if sign > 0:
-            return pl.ds(cz_n - b, b - a + 1), pl.ds(deep - b - base, b - a + 1)
-        return pl.ds(a - 1, b - a + 1), pl.ds(cz_n + a - 1 - base, b - a + 1)
+            return pl.ds(cz_n - b, b - a + 1), pl.ds(deep - b, b - a + 1)
+        return pl.ds(a - 1, b - a + 1), pl.ds(cz_n + a - 1, b - a + 1)
 
     lots = []
 
@@ -130,50 +130,36 @@
     def arrive(i):
         settle(near_r.at[i], lots[i])
 
-    def to_corners(src, dst, halo, n, base=0):
+    def to_corners(src, dst, halo, n, land=None):
+        land = halo if land is None else land
         for to, sx, sz in zip(corners, (1, 1, -1, -1), (1, -1, 1, -1)):
-            (fx, tx), (fz, tz) = side_x(sx, halo, 1, n), side_z(sz, 1, n, base)
-            ship(src, dst, to, (fx, fz), (tx, tz))
-
-    def to_z(src, dst, halo, a, b, ways=(1, -1), base=0):
+            fz, tz = side_z(sz, 1, n)
+            ship(src, dst, to, (side_x(sx, halo, 1, n)[0], fz), (side_x(sx, land, 1, n)[1], tz))
+
+    def to_z(src, dst, halo, a, b, ways=(1, -1), land=None, start=0, size=cx_n):
+        land = halo if land is None else land
         for sz in ways:
-            fz, tz = side_z(sz, a, b, base)
-            x = pl.ds(halo, cx_n)
-            ship(src, dst, north if sz > 0 else south, (x, fz), (x, tz))
-
-    def to_x(src, dst, halo, a, b, ways=(1, -1)):
+            fz, tz = side_z(sz, a, b)
+            where_from, where_to = (pl.ds(halo + start, size), fz), (pl.ds(land + start, size), tz)
+            ship(src, dst, north if sz > 0 else south, where_from, where_to)
+
+    def to_x(src, dst, halo, a, b, ways=(1, -1), land=None, start=0, size=cz_n):
+        land = halo if land is None else land
         for sx in ways:
-            fx, tx = side_x(sx, halo, a, b)
-            z = pl.ds(0, cz_n)
+            fx, tx = side_x(sx, halo, a, b)[0], side_x(sx, land, a, b)[1]
+            z = pl.ds(start, size)
             ship(src, dst, east if sx > 0 else west, (fx, z), (tx, z))
 
     both = pl.ds(0, 2)
     lots.append(0)
-    to_corners(x0_ref, x0_ref, 3, 1)
-    to_corners(face_ref.at[both], face_ref.at[both], 3, 1)
-    to_z(x0_ref, x0_ref, 3, 1, 2)
-    to_z(face_ref, face_ref, 3, 1, 1)
-    to_z(face_ref.at[1], face_ref.at[1], 3, 2, 2, (1,))
-    to_z(src_ref, src_ref, 2, 1, 1)
-    to_x(x0_ref, x0_ref, 3, 1, 2)
-    to_x(face_ref, face_ref, 3, 1, 1)
-    to_x(face_ref.at[0], face_ref.at[0], 3, 2, 2, (1,))
-    to_x(src_ref, src_ref, 2, 1, 1)
-
-    rest = pl.ds(1, 3)
-    lots.append(0)
-    to_corners(x0_ref, x0_late, 3, 2, cz_n)
-    to_corners(face_ref, face_late, 3, 2, cz_n)
-    to_corners(src_ref, src_late, 2, 1, cz_n)
-    to_z(x0_ref, x0_late, 3, 3, 3, base=cz_n)
-    to_z(src_ref, src_late, 2, 2, 2, base=cz_n)
-    to_z(face_ref, face_late, 3, 2, 2, base=cz_n)
-    to_z(face_ref.at[1], face_late.at[1], 3, 3, 3, (1,), base=cz_n)
-    to_x(x0_ref, x0_ref, 3, 3, 3)
-    to_x(src_ref, src_ref, 2, 2, 2)
-    to_x(face_ref.at[rest], face_ref.at[rest], 3, 2, 2, (1,))
-    to_x(face_ref.at[0], face_ref.at[0], 3, 3, 3, (1,))
-    to_x(face_ref, face_ref, 3, 2, 2, (-1,))
+    to_corners(x0_ref, x0_ref, 2, 1)
+    to_corners(face_ref.at[both], edge_ref, 3, 1, land=1)
+    to_z(x0_ref, x0_ref, 2, 1, 1)
+    to_z(face_ref.at[1], edge_ref.at[1], 3, 1, 1, (1,), land=1)
+    to_z(face_ref.at[0], edge_ref.at[0], 3, 1, 1, land=1, start=cx_n - 1, size=1)
+    to_x(x0_ref, x0_ref, 2, 1, 1)
+    to_x(face_ref.at[0], edge_ref.at[0], 3, 1, 1, (1,), land=1)
+    to_x(face_ref.at[1], edge_ref.at[1], 3, 1, 1, land=1, start=cz_n - 1, size=1)
 
     level = lax.broadcasted_iota(jnp.int32, (rows, ny), 1)
     bottom = level == 0
@@ -183,6 +169,45 @@
 
     def y_next(f):
         return pltpu.roll(f, ny - 1, f.ndim - 1)
+
+    own_z = pl.ds(0, cz_n)
+    own_x = pl.ds(3, cx_n)
+    shelf = lax.broadcasted_iota(jnp.int32, (cz_n, ny), 0)
+    ends = lax.broadcasted_iota(jnp.int32, (cz_n, ny), 1)
+    cy = face_ref[2, own_x, own_z]
+    rim = (ends == 0) | (ends == ny - 1)
+    main = face_ref[3, own_x, own_z] + jnp.where(rim, jnp.broadcast_to(cy[..., ny - 1 :], cy.shape), 0.0)
+    rise = jnp.where(ends == ny - 1, 0.0, cy)
+
+    def within(f):
+        none = jnp.zeros((1, cz_n, ny), jnp.float32)
+        flux_x = face_ref[0, pl.ds(3, cx_n - 1), own_z] * (f[:-1] - f[1:])
+        flux_x = jnp.concatenate([none, flux_x, none], 0)
+        flux_z = face_ref[1, own_x, own_z] * (f - pltpu.roll(f, cz_n - 1, 1))
+        flux_z = jnp.where(shelf == cz_n - 1, 0.0, flux_z)
+        flux_y = rise * (f - y_next(f))
+        total = main * f + (flux_x[1:] - flux_x[:-1])
+        return total + (flux_z - pltpu.roll(flux_z, 1, 1)) + (flux_y - y_prev(flux_y))
+
+    for c in range(3):
+        rho_ref[c, pl.ds(1, cx_n), own_z] = src_ref[c] - within(x0_ref[c, pl.ds(2, cx_n), own_z])
+    to_z(rho_ref, rho_ref, 1, 1, 1)
+    to_x(rho_ref, rho_ref, 1, 1, 1)
+
+    lots.append(0)
+    to_corners(x0_ref, x0_late, 2, 2)
+    to_corners(face_ref, face_ref, 3, 2)
+    to_corners(rho_ref, rho_late, 1, 1, land=2)
+    to_z(rho_ref, rho_late, 1, 2, 2, land=2)
+    for x in (0, cx_n - 1):
+        to_z(x0_ref, x0_late, 2, 2, 2, start=x, size=1)
+    to_z(face_ref, face_ref, 3, 1, 2)
+    to_z(face_ref.at[1], face_ref.at[1], 3, 3, 3, (1,))
+    to_x(rho_ref, rho_late, 1, 2, 2, land=2)
+    for z in (0, cz_n - 1):
+        to_x(x0_ref, x0_late, 2, 2, 2, start=z, size=1)
+    to_x(face_ref, face_ref, 3, 1, 2)
+    to_x(face_ref.at[0], face_ref.at[0], 3, 3, 3, (1,))
 
     eye = lax.broadcasted_iota(jnp.int32, (cz_n, cz_n), 0) == lax.broadcasted_iota(
         jnp.int32, (cz_n, cz_n), 1
@@ -287,14 +312,35 @@
             coef[0, x] = face_ref[3, x + 1] + wall
             coef[1, x] = jnp.where(lid, 0.0, cy)
 
-    prepare(1, cx_n + 3)
+    seam = (slot == cz_n - 1) | (slot == deep - 1)
+
+    def mend(part, f, coef_w, coef_e, coef_z):
+        flux_w, flux_e = coef_w * (f[0] - f[1]), coef_e * (f[-2] - f[-1])
+        flux_z = jnp.where(seam, coef_z * (f - z_roll(f, -1)), 0.0)
+        part = part - (flux_z - z_roll(flux_z, 1))
+        return jnp.concatenate(
+            [
+                (part[0] - flux_w)[None], (part[1] + flux_w)[None], part[2:-2],
+                (part[-2] - flux_e)[None], (part[-1] + flux_e)[None],
+            ], 0,
+        )
+
+    tail = pl.ds(cz_n, 8)
+    coef_w = edge_ref[0, 0]
+    coef_e = jnp.concatenate([face_ref[0, cx_n + 2, own_z], edge_ref[0, cx_n, tail]], 0)
+    coef_z = jnp.concatenate(
+        [edge_ref[1, pl.ds(0, 1), own_z], face_ref[1, own_x, own_z], edge_ref[1, pl.ds(cx_n + 1, 1), own_z]], 0
+    )
+    coef_z = jnp.concatenate([coef_z, edge_ref[1, :, tail]], 1)
     dots = []
     for c in range(3):
-        r = src_ref[c, pl.ds(1, cx_n + 2)] - apply(x0_ref[c, pl.ds(1, cx_n + 4)])
+        r = mend(rho_ref[c], x0_ref[c, pl.ds(1, cx_n + 2)], coef_w, coef_e, coef_z)
         r_own = own(r)
-        v = apply(r)
+        v = jnp.concatenate([-within(r[1:-1, :cz_n]), jnp.zeros((cx_n, 8, ny), jnp.float32)], 1)
+        none = jnp.zeros((1, deep, ny), jnp.float32)
+        v = -mend(jnp.concatenate([none, v, none], 0), r, coef_w, coef_e, coef_z)
         v_own = own(v)
-        vk_ref[c, pl.ds(3, cx_n), pl.ds(0, cz_n)] = v[:, :cz_n]
+        vk_ref[c, pl.ds(3, cx_n), own_z] = v[1:-1, :cz_n]
         dots.append([(r_own, r_own), (r_own, v_own)])
     lots.append(0)
     to_corners(vk_ref, vk_ref, 3, 2)
@@ -304,38 +350,37 @@
     to_x(vk_ref, vk_ref, 3, 2, 3)
 
     arrive(1)
-    beyond = pl.ds(cz_n, 8)
-    nearest = (slot[cz_n:] == cz_n) | (slot[cz_n:] == deep - 1)
-    farthest = (slot[cz_n:] == cz_n + 2) | (slot[cz_n:] == deep - 3)
-    middle = pl.ds(3, cx_n)
-    for f in range(4):
-        face_ref[f, middle, beyond] = jnp.where(
-            nearest, face_ref[f, middle, beyond], face_late[f, middle]
-        )
-        for x in (1, cx_n + 3):
-            face_ref[f, pl.ds(x, 2), beyond] = face_late[f, pl.ds(x, 2)]
     prepare(0, cx_n + 4)
-    inside = pl.ds(2, cx_n)
+    mine = (slot <= cz_n) | (slot == deep - 1)
+    body_rows = slot < cz_n
+
+    def widen(near, far):
+        n = near.shape[0] - 2
+        mid = jnp.where(mine, near[1:-1], far[2:-2])
+        low = jnp.where(body_rows, near[0], far[1])
+        high = jnp.where(body_rows, near[n + 1], far[n + 2])
+        return jnp.concatenate([far[:1], low[None], mid, high[None], far[-1:]], 0)
+
+    coef_w, coef_e = face_ref[0, 2], face_ref[0, cx_n + 2]
+    coef_z = face_ref[1, pl.ds(1, cx_n + 4)]
     for c in range(3):
-        x0_ref[c, middle, beyond] = jnp.where(
-            farthest, x0_late[c, middle], x0_ref[c, middle, beyond]
-        )
-        for x in (1, cx_n + 3):
-            x0_ref[c, pl.ds(x, 2), beyond] = x0_late[c, pl.ds(x, 2)]
-        src_ref[c, inside, beyond] = jnp.where(
-            nearest, src_ref[c, inside, beyond], src_late[c, inside]
-        )
-        for x in (1, cx_n + 2):
-            src_ref[c, x, beyond] = src_late[c, x]
-        r = src_ref[c] - apply(x0_ref[c])
+        r = widen(rho_ref[c], rho_late[c])
+        f = widen(x0_ref[c, pl.ds(1, cx_n + 2)], x0_late[c])
+        flux_w, flux_e = coef_w * (f[1] - f[2]), coef_e * (f[-3] - f[-2])
+        flux_z = jnp.where(seam, coef_z * (f - z_roll(f, -1)), 0.0)
+        r = r - (flux_z - z_roll(flux_z, 1))
+        r = jnp.concatenate(
+            [
+                r[:1], (r[1] - flux_w)[None], (r[2] + flux_w)[None], r[3:-3],
+                (r[-3] - flux_e)[None], (r[-2] + flux_e)[None], r[-1:],
+            ], 0,
+        )
         res_ref[c] = r
         v_ref[c] = apply(r)
 
     arrive(3)
     m0, m1 = sums_end(0, 2)
     sigma = m1 / m0
-    mine = (slot <= cz_n) | (slot == deep - 1)
-    body_rows = slot < cz_n
     dots = []
     for c in range(3):
         s = sigma[c : c + 1]
@@ -410,7 +455,7 @@
     speed = []
     for c in range(3):
         w = [k[c : c + 1] for k in weight]
-        field = x0_ref[c, pl.ds(2, cx_n + 2)] + w[0] * res_ref[c, pl.ds(1, cx_n + 2)]
+        field = x0_ref[c, pl.ds(1, cx_n + 2)] + w[0] * res_ref[c, pl.ds(1, cx_n + 2)]
         field += w[1] * a1_ref[c] + w[2] * a2_ref[c] + w[3] * a3_ref[c]
         vel_ref[c] = field[1:-1, :cz_n]
         speed.append(field)
@@ -559,15 +604,16 @@
         return vmem((fields, cx_n + 2 * halo, deep, ny), f32)
 
     scratch = [
-        block(3, 3),
         block(3, 2),
+        vmem((3, cx_n, cz_n, ny), f32),
         block(4, 3),
         vmem(bc_flags.shape, jnp.int32),
         vmem((rows, ny), jnp.int32),
         vmem(coarse_inverse.shape, f32),
-        vmem((3, cx_n + 6, 8, ny), f32),
-        vmem((3, cx_n + 4, 8, ny), f32),
-        vmem((4, cx_n + 6, 8, ny), f32),
+        block(3, 2),
+        block(3, 1),
+        block(3, 2),
+        block(2, 1),
         block(2, 2),
         block(3, 2),
         block(3, 1),

time: 30.5 us -> 29.2 us (0.957)
  Pallas kernels: 29.7 us -> 28.4 us
    pallas_call x1, Pallas kernels: 29 us -> 27.7 us  [body(): pl.pallas_call(functools.partial(kernel, (n_gx, n_gz, cx_n, cz_n, ny, lan...]
where the time goes in v5:
time: 29.2 us; the launch traced here: 29.1 us
  Pallas kernels  28.4 us (97%)
  between operations  0.64 us (2%)
    pallas_call x1, Pallas kernels, body(): pl.pallas_call(functools.partial(kernel, (n_gx, n_gz, cx_n, cz_n, ny, lan...  27.7 us
    pallas_call x1, Pallas kernels, body(): pl.pallas_call(put, out_shape=(jax.ShapeDtypeStruct(velocity.shape, f32),...  0.71 us

profile of v5, /device:TPU:0, one launch (start us, length us, event | category | flops | bytes accessed | tf_op | source)
XLA Modules:
  0.0 29.1 jit_solution(7055361340629000689)
XLA Ops:
  0.6 27.7 %corrector.1 = (f32[3,8,16,128]{3,2,1,0:T(8,128)S(1)}, f32[8,16,128]{2,1,0:T(8,128)S(1)}) custom-call(f32[3,8,16,128]{3,2,1,0:T(8,128)} %x0_in.1, f32[3,8,16,128]{3,2,1,0:T(8,128)} %src_in.1, f32[8,16,128]{2,1,0:T(8,128)} %diag_in.1, f32[3,8,16,128]{3,2,1,0:T(8,128)} %face_in.1, s32[2,8,16]{2,1,0:T(8,128)} %bc_in.1, s32[128,128]{1,0:T(8,128)} %bitcast.1, ...), custom_call_target="tpu_custom_call" | custom-call | tf_op jit(solution)/shard_map/corrector/pallas_call | solution.py:647
  28.4 0.7 %put.1 = (f32[3,8,16,128]{3,2,1,0:T(8,128)}, f32[8,16,128]{2,1,0:T(8,128)}) custom-call(f32[3,8,16,128]{3,2,1,0:T(8,128)S(1)} %get-tuple-element.4.a_ref, f32[8,16,128]{2,1,0:T(8,128)S(1)} %get-tuple-element.5.b_ref), custom_call_target="tpu_custom_call" | custom-call | tf_op jit(solution)/shard_map/put/pallas_call | solution.py:674

commit v6 on v5

--- a/solution.py
+++ b/solution.py
@@ -23,9 +23,9 @@
     x0_ref, src_ref, face_ref, bc_ref, map_ref, inv_ref,
     x0_late, rho_ref, rho_late, edge_ref,
     coef, res_ref, v_ref, vk_ref, a1_ref, a2_ref, a3_ref,
-    code_ref, cell_ref, pd_ref, share_ref, q_ref, inv_w, inv_e,
+    code_ref, cell_ref, pd_ref, share_ref, q_ref, inv_side,
     msg, got, msg_z, got_z, msg_c, got_c,
-    tally, near_s, near_r, sum_sem, coarse_sem, load_sem, side_s, side_r,
+    tally, sent, near_r, sum_sem, coarse_sem, load_sem, side_s, side_r,
 ):
     n_gx, n_gz, cx_n, cz_n, ny, lanes = dims
     rows = cx_n * cz_n
@@ -91,12 +91,12 @@
         return ref.at[..., pl.ds(halo, cx_n), pl.ds(0, cz_n), :]
 
     loads = [
-        pltpu.make_async_copy(a, b, load_sem.at[max(0, i - 3)])
+        pltpu.make_async_copy(a, b, load_sem.at[max(0, i - 4)])
         for i, (a, b) in enumerate(
             [
                 (x0_in, inner(x0_ref, 2)), (face_in, inner(face_ref.at[pl.ds(0, 3)], 3)),
                 (diag_in, inner(face_ref.at[3], 3)), (src_in, src_ref),
-                (bc_in, bc_ref), (map_in, map_ref), (inv_in, inv_ref),
+                (map_in, map_ref), (bc_in, bc_ref), (inv_in, inv_ref),
             ]
         )
     ]
@@ -105,7 +105,7 @@
         pl.semaphore_signal(barrier, inc=1, device_id=other, device_id_type=MESH)
     for load in loads:
         load.start()
-    settle(load_sem.at[0], 10 * rows)
+    settle(load_sem.at[0], 11 * rows)
     pl.semaphore_wait(barrier, len(partners))
 
 
@@ -120,12 +120,13 @@
         return pl.ds(a - 1, b - a + 1), pl.ds(cz_n + a - 1, b - a + 1)
 
     lots = []
+    extra = []
 
     def ship(src, dst, to, where_from, where_to):
         target = dst.at[(..., *where_to, slice(None))]
         lots[-1] += math.prod(target.shape[:-1])
         i = len(lots) - 1
-        send(src.at[(..., *where_from, slice(None))], target, near_s.at[i], near_r.at[i], to)
+        send(src.at[(..., *where_from, slice(None))], target, sent.at[0], near_r.at[i], to)
 
     def arrive(i):
         settle(near_r.at[i], lots[i])
@@ -226,11 +227,11 @@
 
     def scatter(msg, got, sem, others):
         for d, to in enumerate(others):
-            send(msg, got.at[d], sem.at[0], sem.at[1], to)
+            send(msg, got.at[d], sent.at[0], sem, to)
+        extra.append(math.prod(got.shape) // ny)
 
     def gathered(msg, got, sem):
-        for k in range(2):
-            pltpu.make_async_copy(got, got, sem.at[k]).wait()
+        pltpu.make_async_copy(got, got, sem).wait()
         return msg[...] + jnp.sum(got[...], axis=0)
 
     def z_roll(f, shift):
@@ -288,7 +289,7 @@
     slot = lax.broadcasted_iota(jnp.int32, (deep, ny), 0)
     floor = lax.broadcasted_iota(jnp.int32, (deep, ny), 1) == 0
     lid = lax.broadcasted_iota(jnp.int32, (deep, ny), 1) == ny - 1
-    for load in loads[4:]:
+    for load in loads[5:]:
         load.wait()
     flag = jnp.where(bottom, column(0), 0) + jnp.where(top, column(1), 0)
     code = map_ref[...] + COARSE * flag
@@ -298,10 +299,8 @@
     to_corners(code_ref, code_ref, 2, 1)
     to_z(code_ref, code_ref, 2, 1, 2)
     to_x(code_ref, code_ref, 2, 1, 2)
-    blocks = [
-        send(inv_ref, inv_w, side_s.at[0], side_r.at[0], east),
-        send(inv_ref, inv_e, side_s.at[1], side_r.at[1], west),
-    ]
+    for k, to in enumerate((east, west)):
+        send(inv_ref, inv_side.at[k], side_s.at[0], side_r.at[0], to)
 
     arrive(0)
 
@@ -342,10 +341,10 @@
         v_own = own(v)
         vk_ref[c, pl.ds(3, cx_n), own_z] = v[1:-1, :cz_n]
         dots.append([(r_own, r_own), (r_own, v_own)])
+    zero = jnp.zeros((8, ny), jnp.float32)
+    sums_start(0, [p for d in dots for p in d + [(zero, zero)] * (PAD - 2)])
     lots.append(0)
     to_corners(vk_ref, vk_ref, 3, 2)
-    zero = jnp.zeros((8, ny), jnp.float32)
-    sums_start(0, [p for d in dots for p in d + [(zero, zero)] * (PAD - 2)])
     to_z(vk_ref, vk_ref, 3, 2, 3)
     to_x(vk_ref, vk_ref, 3, 2, 3)
 
@@ -406,8 +405,8 @@
         a3_ref[c] = a3
     sums_start(1, dots)
     arrive(2)
-    for block in blocks:
-        block.wait()
+    for sem in (side_s, side_r):
+        pltpu.make_async_copy(inv_side, inv_side, sem.at[0]).wait()
     for x in range(cx_n + 4):
         mark = code_ref[x] >= COARSE
         edge = floor | lid
@@ -526,19 +525,16 @@
             for place, col in zip(places, cols)
         )
         msg_c[k] = jnp.sum(line, axis=0, keepdims=True)
-    scatter(msg_c, got_c, coarse_sem, [at(o) for o in spread_to])
-
-    for i in range(4):
-        settle(near_s.at[i], lots[i])
+    scatter(msg_c, got_c, coarse_sem.at[0], [at(o) for o in spread_to])
+
     arrive(4)
     ext = q_ref[...]
     q = 2.0 * ext[1:-1] - shares(2) * smooth(ext)
     q = q[1:-1] + ext[2:-2] - shares(1) * smooth(q)
     q = q[1:-1] + ext[3:-3] - shares(0) * smooth(q)
 
-    settle(near_s.at[4], lots[4])
-    for k in range(2):
-        pltpu.make_async_copy(got_c, got_c, coarse_sem.at[k]).wait()
+    pltpu.make_async_copy(got_c, got_c, coarse_sem.at[0]).wait()
+    settle(sent.at[0], sum(lots) + sum(extra))
 
     def restricted(t):
         rows_in = [
@@ -555,21 +551,27 @@
             out.append(jnp.broadcast_to(col, (COARSE, ny)))
         return out
 
-    def lift(cell, pick):
-        add = jnp.broadcast_to(pick(0), cell.shape)
-        for m in range(1, COARSE):
-            add = jnp.where(cell == m, pick(m), add)
-        return add
-
-    corr = [corrections(inv, restricted(t)) for inv, t in zip((inv_w, inv_ref, inv_e), (-1, 0, 1))]
+    def lift(cell, table):
+        flat = cell.reshape(-1, 8, ny)
+        picked = []
+        for t in range(flat.shape[0]):
+            index = flat[t]
+            low = jnp.bitwise_and(index, 7)
+            value = jnp.take_along_axis(table[:8], low, axis=0)
+            for m in range(8, COARSE, 8):
+                value = jnp.where(index >= m, jnp.take_along_axis(table[m : m + 8], low, axis=0), value)
+            picked.append(value[None])
+        return jnp.concatenate(picked, 0).reshape(cell.shape)
+
+    corr = [corrections(inv, restricted(t)) for inv, t in zip((inv_side.at[0], inv_ref, inv_side.at[1]), (-1, 0, 1))]
     half = lax.broadcasted_iota(jnp.int32, (8, ny), 0) < 4
     spans = (pl.ds(0, 2), pl.ds(2, cx_n), pl.ds(cx_n + 2, 2))
     raised = []
     for k in range(3):
         cell = cell_ref[spans[k]]
-        inside = lift(cell[:, :cz_n], lambda m: corr[k][1][m : m + 1])
-        outside = lift(
-            cell[:, cz_n:], lambda m: jnp.where(half, corr[k][2][m : m + 1], corr[k][0][m : m + 1])
+        inside = lift(cell[:, :cz_n], corr[k][1])
+        outside = jnp.where(
+            half, lift(cell[:, cz_n:], corr[k][2]), lift(cell[:, cz_n:], corr[k][0])
         )
         raised.append(jnp.concatenate([inside, outside], 1))
     e = jnp.concatenate(raised, 0)
@@ -626,22 +628,21 @@
         vmem((cx_n + 4, deep, ny), f32),
         vmem((cx_n + 4, deep, ny), f32),
         vmem((cx_n + 6, deep, ny), f32),
-        vmem(coarse_inverse.shape, f32),
-        vmem(coarse_inverse.shape, f32),
+        vmem((2,) + coarse_inverse.shape, f32),
         vmem((2, 1, 128), f32),
         vmem((2, n_sum, 1, 128), f32),
         vmem((2, 1, 128), f32),
         vmem((2, n_gz - 1, 1, 128), f32),
         vmem((3, 1, lanes), f32),
         vmem((n_spread, 3, 1, lanes), f32),
-        vmem((2048, ny), f32),
+        vmem((4096, ny), f32),
+        dma((1,)),
         dma((5,)),
-        dma((5,)),
-        dma((2, 2, 2) if n_sum < n_gx * n_gz - 1 else (2, 1, 2)),
-        dma((2,)),
-        dma((4,)),
-        dma((2,)),
-        dma((2,)),
+        dma((2, 2) if n_sum < n_gx * n_gz - 1 else (2, 1)),
+        dma((1,)),
+        dma((3,)),
+        dma((1,)),
+        dma((1,)),
     ]
     spec = pl.BlockSpec(memory_space=pltpu.VMEM)
     velocity, pressure = pl.pallas_call(

time: 29.2 us -> 28.8 us (0.986)
  Pallas kernels: 28.4 us -> 28 us
    pallas_call x1, Pallas kernels: 27.7 us -> 27.3 us  [body(): pl.pallas_call(functools.partial(kernel, (n_gx, n_gz, cx_n, cz_n, ny, lan...]
where the time goes in v6:
time: 28.8 us; the launch traced here: 28.7 us
  Pallas kernels  28 us (97%)
  between operations  0.64 us (2%)
    pallas_call x1, Pallas kernels, body(): pl.pallas_call(functools.partial(kernel, (n_gx, n_gz, cx_n, cz_n, ny, lan...  27.3 us
    pallas_call x1, Pallas kernels, body(): pl.pallas_call(put, out_shape=(jax.ShapeDtypeStruct(velocity.shape, f32),...  0.71 us

profile of v6, /device:TPU:0, one launch (start us, length us, event | category | flops | bytes accessed | tf_op | source)
XLA Modules:
  0.0 28.7 jit_solution(13699913600638547306)
XLA Ops:
  0.6 27.3 %corrector.1 = (f32[3,8,16,128]{3,2,1,0:T(8,128)S(1)}, f32[8,16,128]{2,1,0:T(8,128)S(1)}) custom-call(f32[3,8,16,128]{3,2,1,0:T(8,128)} %x0_in.1, f32[3,8,16,128]{3,2,1,0:T(8,128)} %src_in.1, f32[8,16,128]{2,1,0:T(8,128)} %diag_in.1, f32[3,8,16,128]{3,2,1,0:T(8,128)} %face_in.1, s32[2,8,16]{2,1,0:T(8,128)} %bc_in.1, s32[128,128]{1,0:T(8,128)} %bitcast.1, ...), custom_call_target="tpu_custom_call" | custom-call | tf_op jit(solution)/shard_map/corrector/pallas_call | solution.py:648
  28.0 0.7 %put.1 = (f32[3,8,16,128]{3,2,1,0:T(8,128)}, f32[8,16,128]{2,1,0:T(8,128)}) custom-call(f32[3,8,16,128]{3,2,1,0:T(8,128)S(1)} %get-tuple-element.4.a_ref, f32[8,16,128]{2,1,0:T(8,128)S(1)} %get-tuple-element.5.b_ref), custom_call_target="tpu_custom_call" | custom-call | tf_op jit(solution)/shard_map/put/pallas_call | solution.py:675

commit v7 on v6

--- a/solution.py
+++ b/solution.py
@@ -63,22 +63,25 @@
         return (d % n_gx, k % n_gz)
 
     around = {fold(d, k) for d in (-1, 0, 1) for k in (-1, 0, 1)} - {(0, 0)}
-    spread_to = sorted({fold(d, k) for d in range(-2, 3) for k in range(n_gz)} - {(0, 0)})
+    spread_to = sorted({fold(d, k) for d in range(-2, 3) for k in range(n_gz)} - {(0, 0)}, key=lambda o: (o[1] == 0, min(o[1], n_gz - o[1]), -min(o[0], n_gx - o[0])))
     every = {(d, k) for d in range(n_gx) for k in range(n_gz)}
     if direct:
         sum_to = [
             (d, k)
-            for k in sorted(range(n_gz), key=lambda k: -min(k, n_gz - k))
-            for d in sorted(range(n_gx), key=lambda d: -min(d, n_gx - d))
+            for k in sorted(range(n_gz), key=lambda k: (k == 0, min(k, n_gz - k)))
+            for d in sorted(range(n_gx), key=lambda d: (d == 0, d % 4 == 0, d % 2))
             if d or k
         ]
         met = set(around)
-        while True:
-            seen = met | {fold(a + d, b + k) for a, b in around for d, k in met} | {(0, 0)}
-            left = sorted(every - seen, key=lambda o: (min(o[1], n_gz - o[1]), o))
-            if not left:
-                break
-            met |= {left[0], fold(-left[0][0], -left[0][1])}
+
+        def known(extra):
+            reach = met | extra
+            return reach | {fold(a + d, b + k) for a, b in around for d, k in reach} | {(0, 0)}
+
+        while every - known(set()):
+            pairs = [{o, fold(-o[0], -o[1])} for o in sorted(every - met - {(0, 0)})]
+            gain = len(known(set()))
+            met |= max(pairs, key=lambda p: (len(known(p)) - gain) / len(p))
         sum_to = [at(o) for o in sum_to]
     else:
         sum_to = row_x
@@ -252,8 +255,17 @@
         h = (f.shape[0] - cx_n) // 2
         return f[h : h + cx_n, :cz_n].reshape(rows, ny)
 
-    def pack(pairs):
-        sums = [jnp.sum(a * b, axis=0, keepdims=True) for a, b in pairs]
+    def products(fields, pairs):
+        sums = [None] * len(pairs)
+        for p in range(0, rows, 8):
+            tile = [f[p : p + 8] for f in fields]
+            for k, (a, b) in enumerate(pairs):
+                term = tile[a] * tile[b]
+                sums[k] = term if sums[k] is None else sums[k] + term
+        return sums
+
+    def pack(sums):
+        sums = [jnp.sum(s, axis=0, keepdims=True) for s in sums]
         while len(sums) < 3 * PAD:
             sums.append(jnp.zeros_like(sums[0]))
         total = jnp.sum(jnp.concatenate(sums, 0), axis=1, keepdims=True)
@@ -331,6 +343,7 @@
         [edge_ref[1, pl.ds(0, 1), own_z], face_ref[1, own_x, own_z], edge_ref[1, pl.ds(cx_n + 1, 1), own_z]], 0
     )
     coef_z = jnp.concatenate([coef_z, edge_ref[1, :, tail]], 1)
+    zero = jnp.zeros((8, ny), jnp.float32)
     dots = []
     for c in range(3):
         r = mend(rho_ref[c], x0_ref[c, pl.ds(1, cx_n + 2)], coef_w, coef_e, coef_z)
@@ -340,9 +353,8 @@
         v = -mend(jnp.concatenate([none, v, none], 0), r, coef_w, coef_e, coef_z)
         v_own = own(v)
         vk_ref[c, pl.ds(3, cx_n), own_z] = v[1:-1, :cz_n]
-        dots.append([(r_own, r_own), (r_own, v_own)])
-    zero = jnp.zeros((8, ny), jnp.float32)
-    sums_start(0, [p for d in dots for p in d + [(zero, zero)] * (PAD - 2)])
+        dots += products([r_own, v_own], [(0, 0), (0, 1)]) + [zero] * (PAD - 2)
+    sums_start(0, dots)
     lots.append(0)
     to_corners(vk_ref, vk_ref, 3, 2)
     to_z(vk_ref, vk_ref, 3, 2, 3)
@@ -396,10 +408,10 @@
         a2 = (u - s * v) - s * a1
         a3 = apply(a2) - s * a2[1:-1]
         a4 = apply(a3) - s * a3[1:-1]
-        r0, b1, b2, b3, b4 = own(r), own(a1), own(a2), own(a3), own(a4)
-        dots += [
-            (r0, b1), (b1, b1), (b1, b2), (b2, b2), (b2, b3), (b3, b3), (b3, b4), (b4, b4)
-        ]
+        dots += products(
+            [own(r), own(a1), own(a2), own(a3), own(a4)],
+            [(0, 1), (1, 1), (1, 2), (2, 2), (2, 3), (3, 3), (3, 4), (4, 4)],
+        )
         a1_ref[c] = a1[1:-1]
         a2_ref[c] = a2[1:-1]
         a3_ref[c] = a3

time: 28.8 us -> 28.7 us (level)
  no operation moved by 1% of the time
where the time goes in v7:
time: 28.7 us; the launch traced here: 28.5 us
  Pallas kernels  27.9 us (97%)
  between operations  0.64 us (2%)
    pallas_call x1, Pallas kernels, body(): pl.pallas_call(functools.partial(kernel, (n_gx, n_gz, cx_n, cz_n, ny, lan...  27.2 us
    pallas_call x1, Pallas kernels, body(): pl.pallas_call(put, out_shape=(jax.ShapeDtypeStruct(velocity.shape, f32),...  0.71 us

profile of v7, /device:TPU:0, one launch (start us, length us, event | category | flops | bytes accessed | tf_op | source)
XLA Modules:
  0.0 28.5 jit_solution(15893888299507002527)
XLA Ops:
  0.6 27.2 %corrector.1 = (f32[3,8,16,128]{3,2,1,0:T(8,128)S(1)}, f32[8,16,128]{2,1,0:T(8,128)S(1)}) custom-call(f32[3,8,16,128]{3,2,1,0:T(8,128)} %x0_in.1, f32[3,8,16,128]{3,2,1,0:T(8,128)} %src_in.1, f32[8,16,128]{2,1,0:T(8,128)} %diag_in.1, f32[3,8,16,128]{3,2,1,0:T(8,128)} %face_in.1, s32[2,8,16]{2,1,0:T(8,128)} %bc_in.1, s32[128,128]{1,0:T(8,128)} %bitcast.1, ...), custom_call_target="tpu_custom_call" | custom-call | tf_op jit(solution)/shard_map/corrector/pallas_call | solution.py:660
  27.8 0.7 %put.1 = (f32[3,8,16,128]{3,2,1,0:T(8,128)}, f32[8,16,128]{2,1,0:T(8,128)}) custom-call(f32[3,8,16,128]{3,2,1,0:T(8,128)S(1)} %get-tuple-element.4.a_ref, f32[8,16,128]{2,1,0:T(8,128)S(1)} %get-tuple-element.5.b_ref), custom_call_target="tpu_custom_call" | custom-call | tf_op jit(solution)/shard_map/put/pallas_call | solution.py:687

commit v8 on v7

--- a/solution.py
+++ b/solution.py
@@ -94,7 +94,7 @@
         return ref.at[..., pl.ds(halo, cx_n), pl.ds(0, cz_n), :]
 
     loads = [
-        pltpu.make_async_copy(a, b, load_sem.at[max(0, i - 4)])
+        pltpu.make_async_copy(a, b, load_sem.at[(0, 0, 1, 1, 1, 2, 3)[i]])
         for i, (a, b) in enumerate(
             [
                 (x0_in, inner(x0_ref, 2)), (face_in, inner(face_ref.at[pl.ds(0, 3)], 3)),
@@ -108,7 +108,7 @@
         pl.semaphore_signal(barrier, inc=1, device_id=other, device_id_type=MESH)
     for load in loads:
         load.start()
-    settle(load_sem.at[0], 11 * rows)
+    settle(load_sem.at[0], 6 * rows)
     pl.semaphore_wait(barrier, len(partners))
 
 
@@ -174,6 +174,7 @@
     def y_next(f):
         return pltpu.roll(f, ny - 1, f.ndim - 1)
 
+    settle(load_sem.at[1], 5 * rows)
     own_z = pl.ds(0, cz_n)
     own_x = pl.ds(3, cx_n)
     shelf = lax.broadcasted_iota(jnp.int32, (cz_n, ny), 0)
@@ -502,19 +503,22 @@
     full = jnp.concatenate([blank[:1], trace, blank[:1]], 0)
     full = full - smooth(jnp.concatenate([blank, shares(1) * trace, blank], 0))
 
-    part = [[] for _ in range(6)]
-    for m in range(COARSE):
-        hit = jnp.where(cell_ref[...] == m, full, 0.0)
-        flat = hit[:, :cz_n].reshape(-1, 8, ny)
-        step = cz_n // 8
-        top_rows = hit[:, cz_n:]
-        part[0].append(jnp.sum(flat[: 2 * step], axis=0, keepdims=True))
-        part[1].append(jnp.sum(flat[2 * step : -2 * step], axis=0, keepdims=True))
-        part[2].append(jnp.sum(flat[-2 * step :], axis=0, keepdims=True))
-        part[3].append(top_rows[1:2])
-        part[4].append(jnp.sum(top_rows[2:-2], axis=0, keepdims=True))
-        part[5].append(top_rows[-2:-1])
-    part = [jnp.concatenate(p, 0) for p in part]
+    def binned(spots_in):
+        sums = [None] * COARSE
+        for x, z in spots_in:
+            cell, value = cell_ref[x, pl.ds(z, 8)], full[x, z : z + 8]
+            for m in range(COARSE):
+                term = jnp.where(cell == m, value, 0.0)
+                sums[m] = term if sums[m] is None else sums[m] + term
+        return jnp.concatenate([s[None] for s in sums], 0)
+
+    steps = range(0, cz_n, 8)
+    middle = range(2, cx_n + 2)
+    part = [
+        binned([(x, z) for x in span for z in steps])
+        for span in (range(2), middle, range(cx_n + 2, cx_n + 4))
+    ]
+    part += [binned([(x, cz_n) for x in span]) for span in ((1,), middle, (cx_n + 2,))]
     upper_half = lax.broadcasted_iota(jnp.int32, (COARSE, 8, ny), 1) < 4
 
     def total_of(p):
@@ -652,7 +656,7 @@
         dma((5,)),
         dma((2, 2) if n_sum < n_gx * n_gz - 1 else (2, 1)),
         dma((1,)),
-        dma((3,)),
+        dma((4,)),
         dma((1,)),
         dma((1,)),
     ]

time: 28.7 us -> 28.7 us (level)
  no operation moved by 1% of the time
where the time goes in v8:
time: 28.7 us; the launch traced here: 28.5 us
  Pallas kernels  27.9 us (97%)
  between operations  0.64 us (2%)
    pallas_call x1, Pallas kernels, body(): pl.pallas_call(functools.partial(kernel, (n_gx, n_gz, cx_n, cz_n, ny, lan...  27.2 us
    pallas_call x1, Pallas kernels, body(): pl.pallas_call(put, out_shape=(jax.ShapeDtypeStruct(velocity.shape, f32),...  0.71 us

profile of v8, /device:TPU:0, one launch (start us, length us, event | category | flops | bytes accessed | tf_op | source)
XLA Modules:
  0.0 28.5 jit_solution(12946042832004762804)
XLA Ops:
  0.6 27.2 %corrector.1 = (f32[3,8,16,128]{3,2,1,0:T(8,128)S(1)}, f32[8,16,128]{2,1,0:T(8,128)S(1)}) custom-call(f32[3,8,16,128]{3,2,1,0:T(8,128)} %x0_in.1, f32[3,8,16,128]{3,2,1,0:T(8,128)} %src_in.1, f32[8,16,128]{2,1,0:T(8,128)} %diag_in.1, f32[3,8,16,128]{3,2,1,0:T(8,128)} %face_in.1, s32[2,8,16]{2,1,0:T(8,128)} %bc_in.1, s32[128,128]{1,0:T(8,128)} %bitcast.1, ...), custom_call_target="tpu_custom_call" | custom-call | tf_op jit(solution)/shard_map/corrector/pallas_call | solution.py:664
  27.8 0.7 %put.1 = (f32[3,8,16,128]{3,2,1,0:T(8,128)}, f32[8,16,128]{2,1,0:T(8,128)}) custom-call(f32[3,8,16,128]{3,2,1,0:T(8,128)S(1)} %get-tuple-element.4.a_ref, f32[8,16,128]{2,1,0:T(8,128)S(1)} %get-tuple-element.5.b_ref), custom_call_target="tpu_custom_call" | custom-call | tf_op jit(solution)/shard_map/put/pallas_call | solution.py:691
